TPU v7x, 32 devices: a whole 2x2x4 slice. The times are simulated.
32 devices in a mesh: section: 2 (over core), space: 16 (over z, y, x).
Axes of the slice: x: 2, y: 2, z: 4, core: 2. Of those that a mesh axis runs over, the one named last changes fastest.
Arguments:
- feats: bfloat16 [2, 384, 128, 128], P('section', 'space'), may hold values from -6 to 6
- w_first: bfloat16 [2, 27, 128, 128], P('section'), may hold values from -0.109375 to 0.109375
- w_second: bfloat16 [2, 27, 128, 128], P('section'), may hold values from -0.109375 to 0.109375
- w_skip: bfloat16 [27, 128, 128], replicated, may hold values from -0.109375 to 0.109375
- send_tiles: int32 [2, 128, 2], P('section', 'space'), may hold values from 0 to 23
- send_counts: int32 [2, 128], P('section', 'space'), may hold values from 0 to 2, as said below
- neighbours: int32 [2, 27, 384], P('section', None, 'space'), may hold values from 0 to 40, as said below
Outputs:
- outputs: bfloat16 [2, 384, 128, 128], P('section', 'space')
Inputs may be any that keep to these rules, and one draw needn't show every extreme that they name: `send_tiles`: entry [s, p * 8 + d, j] names one of partition p's own tiles. `send_counts`: entry [s, p * 8 + d] is how many slots partition p fills toward its neighbour in direction d; 0 where that neighbour lies outside the grid. `neighbours`: for output tile t of partition q, a value below 24 is q's own tile, 24 + d * 2 + j is slot j of direction d in q's table, 40 is no neighbour; offset 13 names tile t itself.
All inputs are finite; a program needn't handle non-finite values.
Results may differ from a plain program's by a relative error of at most 0.0049.
Values may be sent and summed in bfloat16 or wider, within the bound.
A program may use at most 64 MiB of HBM per device.

v0:
```python
import math

import jax
import jax.numpy as jnp
from jax import lax
from jax.sharding import PartitionSpec as P

GRID_B = 8


step_rows = (-1, -1, -1, 0, 0, 1, 1, 1)
step_cols = (-1, 0, 1, -1, 1, -1, 0, 1)


def shifted(block, axis, distance):
    devices = range(lax.axis_size(axis))
    route = [(i - distance, i) for i in devices if i - distance in devices]
    return lax.ppermute(block, axis, route)


def select_tiles(tile_table, tile_ids):
    entries = tile_table.shape[0]
    selector = (tile_ids[..., None] == jnp.arange(entries, dtype=jnp.int32)).astype(
        tile_table.dtype
    )
    flat_table = tile_table.reshape(entries, -1)
    picked = jnp.dot(selector.reshape(-1, entries), flat_table, preferred_element_type=jnp.float32)
    return picked.astype(tile_table.dtype).reshape(tile_ids.shape + tile_table.shape[1:])


def offsets_batched(tile_table, neighbour_ids, weights):
    tile_count = neighbour_ids.shape[1]
    block_width = math.gcd(tile_count, 8)
    grouped = neighbour_ids.T.reshape(
        tile_count // block_width, block_width, neighbour_ids.shape[0]
    )

    def one_block(block_ids):
        gathered = select_tiles(tile_table, block_ids)
        return jnp.einsum("koc,bkcv->bov", weights, gathered, preferred_element_type=jnp.float32)

    result = lax.map(one_block, grouped)
    return result.reshape((tile_count,) + result.shape[2:])


def route_direct(outgoing):
    groups = []
    for direction in range(len(step_rows)):
        distance = step_rows[direction] * GRID_B + step_cols[direction]
        groups.append(shifted(outgoing[direction], "space", distance))
    return jnp.stack(groups)


def convolve(tile_field, neighbour_ids, weights, send_rows, counts):
    slot_count = send_rows.shape[1]
    live_slot = jnp.arange(slot_count, dtype=jnp.int32)[None, :] < counts[:, None]
    live_rows = jnp.where(live_slot, send_rows, -1)
    outgoing = select_tiles(tile_field, live_rows)
    arrived = route_direct(outgoing)
    arrived = arrived.reshape((-1,) + tile_field.shape[1:])
    zero_tile = jnp.zeros((1,) + tile_field.shape[1:], tile_field.dtype)
    tile_table = jnp.concatenate([tile_field, arrived, zero_tile], axis=0)
    return offsets_batched(tile_table, neighbour_ids, weights)


def local(feats, w_first, w_second, w_skip, send_tiles, send_counts, neighbours):
    neighbour_ids = neighbours[0]
    send_rows = send_tiles[0]
    counts = send_counts[0]
    first_result = jax.nn.relu(
        convolve(feats[0], neighbour_ids, w_first[0], send_rows, counts)
    ).astype(jnp.bfloat16)
    skipped = shifted(first_result, "section", 1)
    joined = jnp.concatenate([first_result, skipped], axis=1)
    joined_weights = jnp.concatenate([w_second[0], w_skip], axis=2)
    second_result = jax.nn.relu(
        convolve(joined, neighbour_ids, joined_weights, send_rows, counts)
    ).astype(jnp.bfloat16)
    return second_result[None]


def solution(mesh):
    placed = (
        P("section", "space", None, None),
        P("section", None, None, None),
        P("section", None, None, None),
        P(),
        P("section", "space", None),
        P("section", "space"),
        P("section", None, "space"),
    )
    return jax.shard_map(
        local,
        mesh=mesh,
        in_specs=placed,
        out_specs=P("section", "space", None, None),
        check_vma=False,
    )
```

profile of v0, /device:TPU:31, one launch (start us, length us, event | category | flops | bytes accessed | tf_op | source)
XLA Modules:
  0.0 170.8 jit_solution(17799886297144370161)
XLA Ops:
  0.0 0.8 copy.16
  1.7 1.8 %convolution_convert_fusion.3 = bf16[16,16384]{1,0:T(8,128)(2,1)S(1)} fusion(bf16[3,8,128,128]{3,2,1,0:T(8,128)(2,1)} %bitcast.222, s32[16]{0:T(128)S(1)} %broadcast_select_fusion), kind=kOutput, calls=%fused_computation.18 | convolution fusion | flops 12845440 | bytes 1310784 | tf_op jit(solution)/shard_map/dot_general | solution.py:27
  3.9 1.9 %collective-permute-start = (bf16[2,128,128]{2,1,0:T(8,128)(2,1)S(1)}, bf16[2,128,128]{2,1,0:T(8,128)(2,1)S(1)}, u32[]{:S(2)}, u32[]{:S(2)}) collective-permute-start(bf16[2,128,128]{2,1,0:T(8,128)(2,1)S(1)} %bitcast.243), channel_id=1, source_target_pairs={{9,0},{10,1},{11,2},{12,3},{13,4},{14,5},{15,6},{25,16},{26,17},{2... | collective-permute-start | bytes 196616 | tf_op jit(solution)/shard_map/ppermute | solution.py:18
  5.9 1.3 collective-permute-start.1
  7.2 1.3 collective-permute-start.2
  8.6 3.1 %collective-permute-start.3 = (bf16[2,128,128]{2,1,0:T(8,128)(2,1)S(1)}, bf16[2,128,128]{2,1,0:T(8,128)(2,1)S(1)}, u32[]{:S(2)}, u32[]{:S(2)}) collective-permute-start(bf16[2,128,128]{2,1,0:T(8,128)(2,1)S(1)} %bitcast.240), channel_id=1, source_target_pairs={{1,0},{2,1},{3,2},{4,3},{5,4},{6,5},{7,6},{8,7},{9,8},{10,9},{11,1... | collective-permute-start | bytes 196616 | tf_op jit(solution)/shard_map/ppermute | solution.py:18
  11.6 1.3 collective-permute-start.4
  13.1 1.3 collective-permute-start.5
  14.4 1.3 collective-permute-start.6
  15.7 1.3 collective-permute-start.7
  17.1 2.8 %collective-permute-done.5 = bf16[2,128,128]{2,1,0:T(8,128)(2,1)S(1)} collective-permute-done((bf16[2,128,128]{2,1,0:T(8,128)(2,1)S(1)}, bf16[2,128,128]{2,1,0:T(8,128)(2,1)S(1)}, u32[]{:S(2)}, u32[]{:S(2)}) %collective-permute-start.5) | collective-permute-done | bytes 65568 | tf_op jit(solution)/shard_map/ppermute | solution.py:18
  19.9 3.6 %collective-permute-done.6 = bf16[2,128,128]{2,1,0:T(8,128)(2,1)S(1)} collective-permute-done((bf16[2,128,128]{2,1,0:T(8,128)(2,1)S(1)}, bf16[2,128,128]{2,1,0:T(8,128)(2,1)S(1)}, u32[]{:S(2)}, u32[]{:S(2)}) %collective-permute-start.6) | collective-permute-done | bytes 65568 | tf_op jit(solution)/shard_map/ppermute | solution.py:18
  23.6 5.9 %collective-permute-done.7 = bf16[2,128,128]{2,1,0:T(8,128)(2,1)S(1)} collective-permute-done((bf16[2,128,128]{2,1,0:T(8,128)(2,1)S(1)}, bf16[2,128,128]{2,1,0:T(8,128)(2,1)S(1)}, u32[]{:S(2)}, u32[]{:S(2)}) %collective-permute-start.7) | collective-permute-done | bytes 65568 | tf_op jit(solution)/shard_map/ppermute | solution.py:18
  29.5 1.3 maximum_maximum_fusion.1
  30.8 1.0 broadcast.36.clone
  31.8 32.2 %while.20 = (s32[]{:T(128)}, bf16[3,8,128,128]{2,3,1,0:T(8,128)(2,1)}, s32[3,8,27]{2,1,0:T(8,128)S(1)}, bf16[41,128,128]{2,1,0:T(8,128)(2,1)}, bf16[27,128,128]{2,1,0:T(8,128)(2,1)}, /*index=5*/s32[]{:T(128)}, bf16[]{:T(256)}) while((s32[]{:T(128)}, bf16[3,8,128,128]{2,3,1,0:T(8,128)(2,1)}, s32[3,8,27]{2,1,0:T(8,128)S(1)}, ...), condition=%wide.region_1.2_spmd, body=%wide.region_0.1_spmd.sunk | while | flops 1199710848 | bytes 37131056 | solution.py:42
  31.9 1.5 pad.24
  33.4 1.0 copy.90
  34.5 2.0 %fusion.37 = bf16[27,8,128,128]{3,1,2,0:T(8,128)(2,1)S(1)} fusion(bf16[41,16384]{1,0:T(8,128)(2,1)S(1)} %bitcast.219, s32[216]{0:T(256)S(1)} %eq.97), kind=kOutput, calls=%fused_computation.1.clone.1 | convolution fusion | flops 293741216 | bytes 8422240 | tf_op jit(solution)/shard_map/while/body/eval_jaxpr/dot_general | solution.py:27
  36.5 2.1 %copy.91 = bf16[27,8,128,128]{3,2,1,0:T(8,128)(2,1)S(1)} copy(bf16[27,8,128,128]{3,1,2,0:T(8,128)(2,1)S(1)} %fusion.37) | data formatting | bytes 14155776 | tf_op jit(solution)/shard_map/while
  38.6 3.9 %fusion.38 = bf16[3,8,128,128]{2,3,1,0:T(8,128)(2,1)} fusion(bf16[3,8,128,128]{2,3,1,0:T(8,128)(2,1)} %get-tuple-element.167, s32[]{:T(128)} %get-tuple-element.166, bf16[8,27,128,128]{3,2,1,0:T(8,128)(2,1)S(1)} %bitcast.217, bf16[27,128,128]{2,1,0:T(8,128)(2,1)} %get-tuple-element.177), kind=kOutput, calls=%fused_computation.3.clone.1 | convolution fusion | flops 905969664 | bytes 8487424 | tf_op jit(solution)/shard_map/while/body/eval_jaxpr/koc,bkcv->bov/dot_general | solution.py:40
  42.6 1.5 pad.24
  44.1 1.0 copy.90
  45.2 2.0 %fusion.37 = bf16[27,8,128,128]{3,1,2,0:T(8,128)(2,1)S(1)} fusion(bf16[41,16384]{1,0:T(8,128)(2,1)S(1)} %bitcast.219, s32[216]{0:T(256)S(1)} %eq.97), kind=kOutput, calls=%fused_computation.1.clone.1 | convolution fusion | flops 293741216 | bytes 8422240 | tf_op jit(solution)/shard_map/while/body/eval_jaxpr/dot_general | solution.py:27
  47.2 2.1 %copy.91 = bf16[27,8,128,128]{3,2,1,0:T(8,128)(2,1)S(1)} copy(bf16[27,8,128,128]{3,1,2,0:T(8,128)(2,1)S(1)} %fusion.37) | data formatting | bytes 14155776 | tf_op jit(solution)/shard_map/while
  49.3 3.9 %fusion.38 = bf16[3,8,128,128]{2,3,1,0:T(8,128)(2,1)} fusion(bf16[3,8,128,128]{2,3,1,0:T(8,128)(2,1)} %get-tuple-element.167, s32[]{:T(128)} %get-tuple-element.166, bf16[8,27,128,128]{3,2,1,0:T(8,128)(2,1)S(1)} %bitcast.217, bf16[27,128,128]{2,1,0:T(8,128)(2,1)} %get-tuple-element.177), kind=kOutput, calls=%fused_computation.3.clone.1 | convolution fusion | flops 905969664 | bytes 8487424 | tf_op jit(solution)/shard_map/while/body/eval_jaxpr/koc,bkcv->bov/dot_general | solution.py:40
  53.4 1.5 pad.24
  54.9 1.0 copy.90
  55.9 2.0 %fusion.37 = bf16[27,8,128,128]{3,1,2,0:T(8,128)(2,1)S(1)} fusion(bf16[41,16384]{1,0:T(8,128)(2,1)S(1)} %bitcast.219, s32[216]{0:T(256)S(1)} %eq.97), kind=kOutput, calls=%fused_computation.1.clone.1 | convolution fusion | flops 293741216 | bytes 8422240 | tf_op jit(solution)/shard_map/while/body/eval_jaxpr/dot_general | solution.py:27
  57.9 2.1 %copy.91 = bf16[27,8,128,128]{3,2,1,0:T(8,128)(2,1)S(1)} copy(bf16[27,8,128,128]{3,1,2,0:T(8,128)(2,1)S(1)} %fusion.37) | data formatting | bytes 14155776 | tf_op jit(solution)/shard_map/while
  60.1 3.9 %fusion.38 = bf16[3,8,128,128]{2,3,1,0:T(8,128)(2,1)} fusion(bf16[3,8,128,128]{2,3,1,0:T(8,128)(2,1)} %get-tuple-element.167, s32[]{:T(128)} %get-tuple-element.166, bf16[8,27,128,128]{3,2,1,0:T(8,128)(2,1)S(1)} %bitcast.217, bf16[27,128,128]{2,1,0:T(8,128)(2,1)} %get-tuple-element.177), kind=kOutput, calls=%fused_computation.3.clone.1 | convolution fusion | flops 905969664 | bytes 8487424 | tf_op jit(solution)/shard_map/while/body/eval_jaxpr/koc,bkcv->bov/dot_general | solution.py:40
  64.0 1.3 maximum_convert_fusion.1
  65.7 1.3 collective-permute-start.8
  67.0 3.2 %collective-permute-done.8 = bf16[24,128,128]{2,1,0:T(8,128)(2,1)S(1)} collective-permute-done((bf16[24,128,128]{2,1,0:T(8,128)(2,1)S(1)}, bf16[24,128,128]{2,1,0:T(8,128)(2,1)S(1)}, u32[]{:S(2)}, u32[]{:S(2)}) %collective-permute-start.8) | collective-permute-done | bytes 786464 | tf_op jit(solution)/shard_map/ppermute | solution.py:18
  70.4 1.2 convolution_convert_fusion.2
  71.6 0.7 slice_bitcast_fusion
  72.4 1.3 collective-permute-start.9
  73.7 1.5 pad_maximum_fusion
  75.2 1.3 collective-permute-start.10
  76.5 1.3 collective-permute-start.11
  77.8 2.1 %collective-permute-start.12 = (bf16[2,256,128]{2,1,0:T(8,128)(2,1)S(1)}, bf16[2,256,128]{2,1,0:T(8,128)(2,1)S(1)}, u32[]{:S(2)}, u32[]{:S(2)}) collective-permute-start(bf16[2,256,128]{2,1,0:T(8,128)(2,1)S(1)} %bitcast.232), channel_id=1, source_target_pairs={{1,0},{2,1},{3,2},{4,3},{5,4},{6,5},{7,6},{8,7},{9,8},{10,9},{11,1... | collective-permute-start | bytes 393224 | tf_op jit(solution)/shard_map/ppermute | solution.py:18
  79.9 1.3 collective-permute-start.13
  81.3 1.3 collective-permute-start.14
  82.7 1.3 collective-permute-start.15
  84.0 1.5 collective-permute-start.16
  85.5 2.4 %collective-permute-done.13 = bf16[2,256,128]{2,1,0:T(8,128)(2,1)S(1)} collective-permute-done((bf16[2,256,128]{2,1,0:T(8,128)(2,1)S(1)}, bf16[2,256,128]{2,1,0:T(8,128)(2,1)S(1)}, u32[]{:S(2)}, u32[]{:S(2)}) %collective-permute-start.13) | collective-permute-done | bytes 131104 | tf_op jit(solution)/shard_map/ppermute | solution.py:18
  88.0 1.4 collective-permute-done.14
  89.5 12.1 %collective-permute-done.15 = bf16[2,256,128]{2,1,0:T(8,128)(2,1)S(1)} collective-permute-done((bf16[2,256,128]{2,1,0:T(8,128)(2,1)S(1)}, bf16[2,256,128]{2,1,0:T(8,128)(2,1)S(1)}, u32[]{:S(2)}, u32[]{:S(2)}) %collective-permute-start.15) | collective-permute-done | bytes 131104 | tf_op jit(solution)/shard_map/ppermute | solution.py:18
  101.6 3.6 %collective-permute-done.16 = bf16[2,256,128]{2,1,0:T(8,128)(2,1)S(1)} collective-permute-done((bf16[2,256,128]{2,1,0:T(8,128)(2,1)S(1)}, bf16[2,256,128]{2,1,0:T(8,128)(2,1)S(1)}, u32[]{:S(2)}, u32[]{:S(2)}) %collective-permute-start.16) | collective-permute-done | bytes 131104 | tf_op jit(solution)/shard_map/ppermute | solution.py:18
  105.2 0.8 maximum_maximum_fusion
  106.2 63.2 %while.21 = (s32[]{:T(128)}, bf16[3,8,128,128]{2,3,1,0:T(8,128)(2,1)S(1)}, s32[3,8,27]{2,1,0:T(8,128)S(1)}, bf16[41,256,128]{2,1,0:T(8,128)(2,1)S(1)}, bf16[27,128,256]{2,1,0:T(8,128)(2,1)}, /*index=5*/s32[]{:T(128)}, bf16[]{:T(256)}) while((s32[]{:T(128)}, bf16[3,8,128,128]{2,3,1,0:T(8,128)(2,1)S(1)}, s32[3,8,27]{2,1,0:T(8,128)S(1)}, ...), condition=%wide.region_3.4_spmd, body=%wide.region_2.3_spmd.sunk | while | flops 2399412736 | bytes 80810320 | solution.py:42
  106.7 2.0 %copy.92 = bf16[6,8,256,128]{3,1,2,0:T(8,128)(2,1)S(1)} copy(bf16[6,8,256,128]{3,2,1,0:T(8,128)(2,1)S(1)} %bitcast.216) | data formatting | bytes 6291456 | tf_op jit(solution)/shard_map/while
  108.7 4.1 %fusion.42 = bf16[27,8,256,128]{3,1,2,0:T(8,128)(2,1)S(1)} fusion(bf16[41,32768]{1,0:T(8,128)(2,1)S(1)} %bitcast.215, s32[216]{0:T(256)S(1)} %eq.101), kind=kOutput, calls=%fused_computation.9.clone.1 | convolution fusion | flops 587473536 | bytes 16843616 | tf_op jit(solution)/shard_map/while/body/eval_jaxpr/dot_general | solution.py:27
  112.8 7.2 %copy.93 = bf16[27,8,256,128]{3,2,1,0:T(8,128)(2,1)} copy(bf16[27,8,256,128]{3,1,2,0:T(8,128)(2,1)S(1)} %fusion.42) | data formatting | bytes 28311552 | tf_op jit(solution)/shard_map/while
  120.0 7.2 %fusion.43 = bf16[3,8,128,128]{2,3,1,0:T(8,128)(2,1)S(1)} fusion(bf16[3,8,128,128]{2,3,1,0:T(8,128)(2,1)S(1)} %get-tuple-element.188, s32[]{:T(128)} %get-tuple-element.187, bf16[8,27,256,128]{3,2,1,0:T(8,128)(2,1)} %bitcast.214, bf16[27,128,256]{2,1,0:T(8,128)(2,1)S(1)} %copy-done.1), kind=kOutput, calls=%fused_computation.13.clone.1 | convolution fusion | flops 1811939328 | bytes 16449540 | tf_op jit(solution)/shard_map/while/body/eval_jaxpr/koc,bkcv->bov/dot_general | solution.py:40
  127.7 2.0 %copy.92 = bf16[6,8,256,128]{3,1,2,0:T(8,128)(2,1)S(1)} copy(bf16[6,8,256,128]{3,2,1,0:T(8,128)(2,1)S(1)} %bitcast.216) | data formatting | bytes 6291456 | tf_op jit(solution)/shard_map/while
  129.8 4.1 %fusion.42 = bf16[27,8,256,128]{3,1,2,0:T(8,128)(2,1)S(1)} fusion(bf16[41,32768]{1,0:T(8,128)(2,1)S(1)} %bitcast.215, s32[216]{0:T(256)S(1)} %eq.101), kind=kOutput, calls=%fused_computation.9.clone.1 | convolution fusion | flops 587473536 | bytes 16843616 | tf_op jit(solution)/shard_map/while/body/eval_jaxpr/dot_general | solution.py:27
  133.9 7.2 %copy.93 = bf16[27,8,256,128]{3,2,1,0:T(8,128)(2,1)} copy(bf16[27,8,256,128]{3,1,2,0:T(8,128)(2,1)S(1)} %fusion.42) | data formatting | bytes 28311552 | tf_op jit(solution)/shard_map/while
  141.1 7.2 %fusion.43 = bf16[3,8,128,128]{2,3,1,0:T(8,128)(2,1)S(1)} fusion(bf16[3,8,128,128]{2,3,1,0:T(8,128)(2,1)S(1)} %get-tuple-element.188, s32[]{:T(128)} %get-tuple-element.187, bf16[8,27,256,128]{3,2,1,0:T(8,128)(2,1)} %bitcast.214, bf16[27,128,256]{2,1,0:T(8,128)(2,1)S(1)} %copy-done.1), kind=kOutput, calls=%fused_computation.13.clone.1 | convolution fusion | flops 1811939328 | bytes 16449540 | tf_op jit(solution)/shard_map/while/body/eval_jaxpr/koc,bkcv->bov/dot_general | solution.py:40
  148.8 2.0 %copy.92 = bf16[6,8,256,128]{3,1,2,0:T(8,128)(2,1)S(1)} copy(bf16[6,8,256,128]{3,2,1,0:T(8,128)(2,1)S(1)} %bitcast.216) | data formatting | bytes 6291456 | tf_op jit(solution)/shard_map/while
  150.9 4.1 %fusion.42 = bf16[27,8,256,128]{3,1,2,0:T(8,128)(2,1)S(1)} fusion(bf16[41,32768]{1,0:T(8,128)(2,1)S(1)} %bitcast.215, s32[216]{0:T(256)S(1)} %eq.101), kind=kOutput, calls=%fused_computation.9.clone.1 | convolution fusion | flops 587473536 | bytes 16843616 | tf_op jit(solution)/shard_map/while/body/eval_jaxpr/dot_general | solution.py:27
  155.0 7.2 %copy.93 = bf16[27,8,256,128]{3,2,1,0:T(8,128)(2,1)} copy(bf16[27,8,256,128]{3,1,2,0:T(8,128)(2,1)S(1)} %fusion.42) | data formatting | bytes 28311552 | tf_op jit(solution)/shard_map/while
  162.2 7.2 %fusion.43 = bf16[3,8,128,128]{2,3,1,0:T(8,128)(2,1)S(1)} fusion(bf16[3,8,128,128]{2,3,1,0:T(8,128)(2,1)S(1)} %get-tuple-element.188, s32[]{:T(128)} %get-tuple-element.187, bf16[8,27,256,128]{3,2,1,0:T(8,128)(2,1)} %bitcast.214, bf16[27,128,256]{2,1,0:T(8,128)(2,1)S(1)} %copy-done.1), kind=kOutput, calls=%fused_computation.13.clone.1 | convolution fusion | flops 1811939328 | bytes 16449540 | tf_op jit(solution)/shard_map/while/body/eval_jaxpr/koc,bkcv->bov/dot_general | solution.py:40
  169.6 1.2 copy.19
  (80 shorter events, 4.4 us)
Async XLA Ops:
  0.0 29.5 %copy-start = (bf16[1,24,128,128]{3,2,1,0:T(8,128)(2,1)S(1)}, bf16[1,24,128,128]{3,2,1,0:T(8,128)(2,1)}, u32[]{:S(2)}) copy-start(bf16[1,24,128,128]{3,2,1,0:T(8,128)(2,1)} %param.11) | copy-start | bytes 2359300
  3.9 9.1 %collective-permute-start = (bf16[2,128,128]{2,1,0:T(8,128)(2,1)S(1)}, bf16[2,128,128]{2,1,0:T(8,128)(2,1)S(1)}, u32[]{:S(2)}, u32[]{:S(2)}) collective-permute-start(bf16[2,128,128]{2,1,0:T(8,128)(2,1)S(1)} %bitcast.243), channel_id=1, source_target_pairs={{9,0},{10,1},{11,2},{12,3},{13,4},{14,5},{15,6},{25,16},{26,17},{2... | collective-permute-start | bytes 196616 | tf_op jit(solution)/shard_map/ppermute | solution.py:18
  5.9 25.9 %copy-start.4 = (s32[1,27,24]{1,2,0:T(8,128)S(1)}, s32[1,27,24]{1,2,0:T(8,128)}, u32[]{:S(2)}) copy-start(s32[1,27,24]{1,2,0:T(8,128)} %param.17) | copy-start | bytes 7780
  5.9 8.5 %collective-permute-start.1 = (bf16[2,128,128]{2,1,0:T(8,128)(2,1)S(1)}, bf16[2,128,128]{2,1,0:T(8,128)(2,1)S(1)}, u32[]{:S(2)}, u32[]{:S(2)}) collective-permute-start(bf16[2,128,128]{2,1,0:T(8,128)(2,1)S(1)} %bitcast.242), channel_id=1, source_target_pairs={{8,0},{9,1},{10,2},{11,3},{12,4},{13,5},{14,6},{15,7},{24,16},{25,... | collective-permute-start | bytes 196616 | tf_op jit(solution)/shard_map/ppermute | solution.py:18
  7.2 8.5 %collective-permute-start.2 = (bf16[2,128,128]{2,1,0:T(8,128)(2,1)S(1)}, bf16[2,128,128]{2,1,0:T(8,128)(2,1)S(1)}, u32[]{:S(2)}, u32[]{:S(2)}) collective-permute-start(bf16[2,128,128]{2,1,0:T(8,128)(2,1)S(1)} %bitcast.241), channel_id=1, source_target_pairs={{7,0},{8,1},{9,2},{10,3},{11,4},{12,5},{13,6},{14,7},{15,8},{23,16... | collective-permute-start | bytes 196616 | tf_op jit(solution)/shard_map/ppermute | solution.py:18
  8.6 8.5 %collective-permute-start.3 = (bf16[2,128,128]{2,1,0:T(8,128)(2,1)S(1)}, bf16[2,128,128]{2,1,0:T(8,128)(2,1)S(1)}, u32[]{:S(2)}, u32[]{:S(2)}) collective-permute-start(bf16[2,128,128]{2,1,0:T(8,128)(2,1)S(1)} %bitcast.240), channel_id=1, source_target_pairs={{1,0},{2,1},{3,2},{4,3},{5,4},{6,5},{7,6},{8,7},{9,8},{10,9},{11,1... | collective-permute-start | bytes 196616 | tf_op jit(solution)/shard_map/ppermute | solution.py:18
  11.6 5.4 %collective-permute-start.4 = (bf16[2,128,128]{2,1,0:T(8,128)(2,1)S(1)}, bf16[2,128,128]{2,1,0:T(8,128)(2,1)S(1)}, u32[]{:S(2)}, u32[]{:S(2)}) collective-permute-start(bf16[2,128,128]{2,1,0:T(8,128)(2,1)S(1)} %bitcast.239), channel_id=1, source_target_pairs={{0,1},{1,2},{2,3},{3,4},{4,5},{5,6},{6,7},{7,8},{8,9},{9,10},{10,1... | collective-permute-start | bytes 196616 | tf_op jit(solution)/shard_map/ppermute | solution.py:18
  13.1 6.8 %collective-permute-start.5 = (bf16[2,128,128]{2,1,0:T(8,128)(2,1)S(1)}, bf16[2,128,128]{2,1,0:T(8,128)(2,1)S(1)}, u32[]{:S(2)}, u32[]{:S(2)}) collective-permute-start(bf16[2,128,128]{2,1,0:T(8,128)(2,1)S(1)} %bitcast.238), channel_id=1, source_target_pairs={{0,7},{1,8},{2,9},{3,10},{4,11},{5,12},{6,13},{7,14},{8,15},{16,23... | collective-permute-start | bytes 196616 | tf_op jit(solution)/shard_map/ppermute | solution.py:18
  14.4 9.2 %collective-permute-start.6 = (bf16[2,128,128]{2,1,0:T(8,128)(2,1)S(1)}, bf16[2,128,128]{2,1,0:T(8,128)(2,1)S(1)}, u32[]{:S(2)}, u32[]{:S(2)}) collective-permute-start(bf16[2,128,128]{2,1,0:T(8,128)(2,1)S(1)} %bitcast.237), channel_id=1, source_target_pairs={{0,8},{1,9},{2,10},{3,11},{4,12},{5,13},{6,14},{7,15},{16,24},{17,... | collective-permute-start | bytes 196616 | tf_op jit(solution)/shard_map/ppermute | solution.py:18
  15.7 13.8 %collective-permute-start.7 = (bf16[2,128,128]{2,1,0:T(8,128)(2,1)S(1)}, bf16[2,128,128]{2,1,0:T(8,128)(2,1)S(1)}, u32[]{:S(2)}, u32[]{:S(2)}) collective-permute-start(bf16[2,128,128]{2,1,0:T(8,128)(2,1)S(1)} %bitcast.236), channel_id=1, source_target_pairs={{0,9},{1,10},{2,11},{3,12},{4,13},{5,14},{6,15},{16,25},{17,26},{1... | collective-permute-start | bytes 196616 | tf_op jit(solution)/shard_map/ppermute | solution.py:18
  65.7 4.5 %collective-permute-start.8 = (bf16[24,128,128]{2,1,0:T(8,128)(2,1)S(1)}, bf16[24,128,128]{2,1,0:T(8,128)(2,1)S(1)}, u32[]{:S(2)}, u32[]{:S(2)}) collective-permute-start(bf16[24,128,128]{2,1,0:T(8,128)(2,1)S(1)} %copy.18), channel_id=1, source_target_pairs={{0,16},{1,17},{2,18},{3,19},{4,20},{5,21},{6,22},{7,23},{8,24},{9,... | collective-permute-start | bytes 2359304 | tf_op jit(solution)/shard_map/ppermute | solution.py:18
  70.3 3.3 %copy-start.2 = (bf16[27,128,128]{2,1,0:T(8,128)(2,1)S(1)}, bf16[27,128,128]{2,1,0:T(8,128)(2,1)}, u32[]{:S(2)}) copy-start(bf16[27,128,128]{2,1,0:T(8,128)(2,1)} %param.14) | copy-start | bytes 2654212
  70.3 3.3 %copy-start.3 = (bf16[1,27,128,128]{3,2,1,0:T(8,128)(2,1)S(1)}, bf16[1,27,128,128]{3,2,1,0:T(8,128)(2,1)}, u32[]{:S(2)}) copy-start(bf16[1,27,128,128]{3,2,1,0:T(8,128)(2,1)} %param.13) | copy-start | bytes 2654212
  72.4 9.0 %collective-permute-start.9 = (bf16[2,256,128]{2,1,0:T(8,128)(2,1)S(1)}, bf16[2,256,128]{2,1,0:T(8,128)(2,1)S(1)}, u32[]{:S(2)}, u32[]{:S(2)}) collective-permute-start(bf16[2,256,128]{2,1,0:T(8,128)(2,1)S(1)} %bitcast.235), channel_id=1, source_target_pairs={{9,0},{10,1},{11,2},{12,3},{13,4},{14,5},{15,6},{25,16},{26,17},{2... | collective-permute-start | bytes 393224 | tf_op jit(solution)/shard_map/ppermute | solution.py:18
  75.2 7.5 %collective-permute-start.10 = (bf16[2,256,128]{2,1,0:T(8,128)(2,1)S(1)}, bf16[2,256,128]{2,1,0:T(8,128)(2,1)S(1)}, u32[]{:S(2)}, u32[]{:S(2)}) collective-permute-start(bf16[2,256,128]{2,1,0:T(8,128)(2,1)S(1)} %bitcast.234), channel_id=1, source_target_pairs={{8,0},{9,1},{10,2},{11,3},{12,4},{13,5},{14,6},{15,7},{24,16},{25,... | collective-permute-start | bytes 393224 | tf_op jit(solution)/shard_map/ppermute | solution.py:18
  76.5 7.5 %collective-permute-start.11 = (bf16[2,256,128]{2,1,0:T(8,128)(2,1)S(1)}, bf16[2,256,128]{2,1,0:T(8,128)(2,1)S(1)}, u32[]{:S(2)}, u32[]{:S(2)}) collective-permute-start(bf16[2,256,128]{2,1,0:T(8,128)(2,1)S(1)} %bitcast.233), channel_id=1, source_target_pairs={{7,0},{8,1},{9,2},{10,3},{11,4},{12,5},{13,6},{14,7},{15,8},{23,16... | collective-permute-start | bytes 393224 | tf_op jit(solution)/shard_map/ppermute | solution.py:18
  77.8 7.7 %collective-permute-start.12 = (bf16[2,256,128]{2,1,0:T(8,128)(2,1)S(1)}, bf16[2,256,128]{2,1,0:T(8,128)(2,1)S(1)}, u32[]{:S(2)}, u32[]{:S(2)}) collective-permute-start(bf16[2,256,128]{2,1,0:T(8,128)(2,1)S(1)} %bitcast.232), channel_id=1, source_target_pairs={{1,0},{2,1},{3,2},{4,3},{5,4},{6,5},{7,6},{8,7},{9,8},{10,9},{11,1... | collective-permute-start | bytes 393224 | tf_op jit(solution)/shard_map/ppermute | solution.py:18
  79.9 8.0 %collective-permute-start.13 = (bf16[2,256,128]{2,1,0:T(8,128)(2,1)S(1)}, bf16[2,256,128]{2,1,0:T(8,128)(2,1)S(1)}, u32[]{:S(2)}, u32[]{:S(2)}) collective-permute-start(bf16[2,256,128]{2,1,0:T(8,128)(2,1)S(1)} %bitcast.231), channel_id=1, source_target_pairs={{0,1},{1,2},{2,3},{3,4},{4,5},{5,6},{6,7},{7,8},{8,9},{9,10},{10,1... | collective-permute-start | bytes 393224 | tf_op jit(solution)/shard_map/ppermute | solution.py:18
  81.3 8.1 %collective-permute-start.14 = (bf16[2,256,128]{2,1,0:T(8,128)(2,1)S(1)}, bf16[2,256,128]{2,1,0:T(8,128)(2,1)S(1)}, u32[]{:S(2)}, u32[]{:S(2)}) collective-permute-start(bf16[2,256,128]{2,1,0:T(8,128)(2,1)S(1)} %bitcast.230), channel_id=1, source_target_pairs={{0,7},{1,8},{2,9},{3,10},{4,11},{5,12},{6,13},{7,14},{8,15},{16,23... | collective-permute-start | bytes 393224 | tf_op jit(solution)/shard_map/ppermute | solution.py:18
  82.7 18.9 %collective-permute-start.15 = (bf16[2,256,128]{2,1,0:T(8,128)(2,1)S(1)}, bf16[2,256,128]{2,1,0:T(8,128)(2,1)S(1)}, u32[]{:S(2)}, u32[]{:S(2)}) collective-permute-start(bf16[2,256,128]{2,1,0:T(8,128)(2,1)S(1)} %bitcast.229), channel_id=1, source_target_pairs={{0,8},{1,9},{2,10},{3,11},{4,12},{5,13},{6,14},{7,15},{16,24},{17,... | collective-permute-start | bytes 393224 | tf_op jit(solution)/shard_map/ppermute | solution.py:18
  84.0 21.2 %collective-permute-start.16 = (bf16[2,256,128]{2,1,0:T(8,128)(2,1)S(1)}, bf16[2,256,128]{2,1,0:T(8,128)(2,1)S(1)}, u32[]{:S(2)}, u32[]{:S(2)}) collective-permute-start(bf16[2,256,128]{2,1,0:T(8,128)(2,1)S(1)} %bitcast.228), channel_id=1, source_target_pairs={{0,9},{1,10},{2,11},{3,12},{4,13},{5,14},{6,15},{16,25},{17,26},{1... | collective-permute-start | bytes 393224 | tf_op jit(solution)/shard_map/ppermute | solution.py:18
  112.8 7.2 %copy-start.1 = (bf16[27,128,256]{2,1,0:T(8,128)(2,1)S(1)}, bf16[27,128,256]{2,1,0:T(8,128)(2,1)}, u32[]{:S(2)}) copy-start(bf16[27,128,256]{2,1,0:T(8,128)(2,1)} %get-tuple-element.198) | copy-start | bytes 5308420 | tf_op jit(solution)/shard_map/while
  133.9 7.2 %copy-start.1 = (bf16[27,128,256]{2,1,0:T(8,128)(2,1)S(1)}, bf16[27,128,256]{2,1,0:T(8,128)(2,1)}, u32[]{:S(2)}) copy-start(bf16[27,128,256]{2,1,0:T(8,128)(2,1)} %get-tuple-element.198) | copy-start | bytes 5308420 | tf_op jit(solution)/shard_map/while
  155.0 7.2 %copy-start.1 = (bf16[27,128,256]{2,1,0:T(8,128)(2,1)S(1)}, bf16[27,128,256]{2,1,0:T(8,128)(2,1)}, u32[]{:S(2)}) copy-start(bf16[27,128,256]{2,1,0:T(8,128)(2,1)} %get-tuple-element.198) | copy-start | bytes 5308420 | tf_op jit(solution)/shard_map/while
where the time goes:
time: 172 us; the launch traced here: 171 us
  matrix products  54.8 us (32%)
  local copies, waits for them, and re-layouts  48.8 us (28%)
  waiting for transfers between devices  35.1 us (20%)
  starting transfers between devices  25.4 us (15%)
  other arithmetic  5.93 us (3%)
    while x24, local copies, waits for them, and re-layouts  42.8 us
    ppermute x17, waiting for transfers between devices, shifted(): return lax.ppermute(block, axis, route)  35.1 us
    dot_general x6, matrix products, one_block(): jnp.einsum('koc,bkcv->bov', weights, gathered, preferred_element_type=jnp...  33.4 us
    ppermute x17, starting transfers between devices, shifted(): return lax.ppermute(block, axis, route)  25.4 us
    dot_general x8, matrix products, select_tiles(): jnp.dot(selector.reshape(-1, entries), flat_table, preferred_element_type...  21.4 us
  transfers between devices with their start and end apart: 17, of which 8 were waited for; matrix products, arithmetic and copies ran while one was open for 1% of the time, Pallas kernels for 0%

commit v1 on v0

v1 whole, which is shorter than its diff:
```python
import jax
import jax.numpy as jnp
from jax import lax
from jax.experimental import pallas as pl
from jax.experimental.pallas import tpu as pltpu
from jax.sharding import PartitionSpec as P

GRID_B = 8

step_rows = (-1, -1, -1, 0, 0, 1, 1, 1)
step_cols = (-1, 0, 1, -1, 1, -1, 0, 1)


def shifted(block, axis, distance):
    devices = range(lax.axis_size(axis))
    route = [(i - distance, i) for i in devices if i - distance in devices]
    return lax.ppermute(block, axis, route)


def conv_tiles(ids, pairs, emit, tiles, koff):
    def body(step, _):
        t = step * 2
        terms = [(w, table, k) for k in range(koff) for w, table in pairs]
        acc = None
        for i in range(0, len(terms), 2):
            lhs, rhs = [], []
            for w, table, k in terms[i : i + 2]:
                lhs.append(w[k])
                rhs.append(jnp.concatenate([table[ids[k, t]], table[ids[k, t + 1]]], axis=1))
            part = jnp.dot(
                jnp.concatenate(lhs, axis=1),
                jnp.concatenate(rhs, axis=0),
                preferred_element_type=jnp.float32,
            )
            acc = part if acc is None else acc + part
        emit(t, acc)
        return 0

    lax.fori_loop(0, tiles // 2, body, 0)


def fill(table, own, arrived):
    tiles, slots = own.shape[0], arrived.shape[0]
    table[pl.ds(0, tiles)] = own[...]
    table[pl.ds(tiles, slots)] = arrived[...]
    table[tiles + slots] = jnp.zeros(table.shape[1:], table.dtype)


def store_relu(out):
    def emit(t, acc):
        vox = out.shape[2]
        acc = jnp.maximum(acc, 0.0).astype(out.dtype)
        out[t] = acc[:, :vox]
        out[t + 1] = acc[:, vox:]

    return emit


def first_kernel(ids, own, arrived, w, out, table):
    fill(table, own, arrived)
    conv_tiles(ids, [(w, table)], store_relu(out), own.shape[0], w.shape[0])


def second_kernel(ids, own, arrived, skip, skip_arrived, w, w_skip, out, table, skip_table):
    fill(table, own, arrived)

    @pl.when(lax.axis_index("section") == 0)
    def _():
        conv_tiles(ids, [(w, table)], store_relu(out), own.shape[0], w.shape[0])

    @pl.when(lax.axis_index("section") == 1)
    def _():
        fill(skip_table, skip, skip_arrived)
        conv_tiles(
            ids, [(w, table), (w_skip, skip_table)], store_relu(out), own.shape[0], w.shape[0]
        )


def select_kernel(rows, counts, *refs):
    fields, outs = refs[: len(refs) // 2], refs[len(refs) // 2 :]
    for field, out in zip(fields, outs):
        for d in range(rows.shape[0]):
            for j in range(rows.shape[1]):
                tile = field[rows[d, j]]
                out[d, j] = jnp.where(j < counts[d], tile, jnp.zeros_like(tile))


VMEM = pl.BlockSpec(memory_space=pltpu.VMEM)
SMEM = pl.BlockSpec(memory_space=pltpu.SMEM)


def halos(fields, send_rows, counts):
    dirs, cap = send_rows.shape
    tile = fields[0].shape[1:]
    outgoing = pl.pallas_call(
        select_kernel,
        out_shape=[jax.ShapeDtypeStruct((dirs, cap) + tile, f.dtype) for f in fields],
        in_specs=[SMEM, SMEM] + [VMEM] * len(fields),
        out_specs=[VMEM] * len(fields),
    )(send_rows, counts, *fields)
    joined = jnp.stack(outgoing, axis=2)
    groups = []
    for direction in range(len(step_rows)):
        distance = step_rows[direction] * GRID_B + step_cols[direction]
        groups.append(shifted(joined[direction], "space", distance))
    arrived = jnp.stack(groups).reshape((dirs * cap, len(fields)) + tile)
    return [arrived[:, i] for i in range(len(fields))]


def local(feats, w_first, w_second, w_skip, send_tiles, send_counts, neighbours):
    ids, send_rows, counts = neighbours[0], send_tiles[0], send_counts[0]
    own = feats[0]
    tiles, channels, vox = own.shape
    slots = send_rows.shape[0] * send_rows.shape[1]
    table = pltpu.VMEM((tiles + slots + 1, channels, vox), own.dtype)
    shape = jax.ShapeDtypeStruct((tiles, channels, vox), own.dtype)
    (arrived,) = halos([own], send_rows, counts)
    first = pl.pallas_call(
        first_kernel,
        out_shape=shape,
        in_specs=[SMEM] + [VMEM] * 3,
        out_specs=VMEM,
        scratch_shapes=[table],
    )(ids, own, arrived, w_first[0])
    skip = shifted(first, "section", 1)
    arrived, skip_arrived = halos([first, skip], send_rows, counts)
    second = pl.pallas_call(
        second_kernel,
        out_shape=shape,
        in_specs=[SMEM] + [VMEM] * 6,
        out_specs=VMEM,
        scratch_shapes=[table, table],
    )(ids, first, arrived, skip, skip_arrived, w_second[0], w_skip)
    return second[None]


def solution(mesh):
    placed = (
        P("section", "space", None, None),
        P("section", None, None, None),
        P("section", None, None, None),
        P(),
        P("section", "space", None),
        P("section", "space"),
        P("section", None, "space"),
    )
    return jax.shard_map(
        local,
        mesh=mesh,
        in_specs=placed,
        out_specs=P("section", "space", None, None),
        check_vma=False,
    )
```

time: 172 us -> 107 us (0.62)
  the two profiles are of different devices: /device:TPU:31 before, /device:TPU:27 now
where the time goes in v1:
time: 107 us
  starting transfers between devices  46.6 us (44%)
  waiting for transfers between devices  29.1 us (27%)
  Pallas kernels  23.2 us (22%)
  local copies, waits for them, and re-layouts  6.26 us (6%)
  other arithmetic  1.33 us (1%)
    ppermute x17, starting transfers between devices, shifted(): return lax.ppermute(block, axis, route)  46.6 us
    ppermute x17, waiting for transfers between devices, shifted(): return lax.ppermute(block, axis, route)  29.1 us
    pallas_call x1, Pallas kernels, local(): pl.pallas_call(second_kernel, out_shape=shape, in_specs=[SMEM] + [VMEM] *...  10.9 us
    pallas_call x1, Pallas kernels, local(): pl.pallas_call(first_kernel, out_shape=shape, in_specs=[SMEM] + [VMEM] *...  7.57 us
    pallas_call x2, Pallas kernels, halos(): pl.pallas_call(select_kernel, out_shape=[jax.ShapeDtypeStruct((dirs, cap)...  4.67 us
    unnamed x23, local copies, waits for them, and re-layouts  3.28 us
  transfers between devices with their start and end apart: 17, of which 6 were waited for; matrix products, arithmetic and copies ran while one was open for 1% of the time, Pallas kernels for 0%

profile of v1, /device:TPU:27, one launch (start us, length us, event | category | flops | bytes accessed | tf_op | source)
XLA Modules:
  0.0 106.8 jit_solution(6367026929508139247)
XLA Ops:
  0.0 0.0 copy-start.3
  0.0 0.7 copy-done.3
  0.7 0.7 copy.9.rows
  1.4 2.1 %shard_map.73 = bf16[8,2,128,128]{3,2,1,0:T(8,128)(2,1)} custom-call(s32[8,2]{1,0:T(8,128)} %copy.9.rows, s32[8]{0:T(128)} %bitcast.103, bf16[24,128,128]{2,1,0:T(8,128)(2,1)} %bitcast.94), custom_call_target="tpu_custom_call" | custom-call | tf_op jit(solution)/shard_map/pallas_call | solution.py:95
  3.4 0.0 copy-start.2
  3.4 1.1 %slice_bitcast_fusion.2 = (bf16[2,1,128,128]{3,2,0,1:T(8,128)(2,1)S(1)}, bf16[2,1,128,128]{3,2,0,1:T(8,128)(2,1)S(1)}, bf16[2,1,128,128]{3,2,0,1:T(8,128)(2,1)S(...) fusion(bf16[8,2,128,128]{3,2,1,0:T(8,128)(2,1)} %shard_map.73), kind=kLoop, calls=%fused_computation.40 | loop fusion | bytes 1048576 | tf_op jit(solution)/shard_map/squeeze | solution.py:105
  4.5 1.9 %collective-permute-start = (bf16[2,1,128,128]{3,2,0,1:T(8,128)(2,1)S(1)}, bf16[2,1,128,128]{3,2,0,1:T(8,128)(2,1)S(1)}, u32[]{:S(2)}, u32[]{:S(2)}) collective-permute-start(bf16[2,1,128,128]{3,2,0,1:T(8,128)(2,1)S(1)} %get-tuple-element.26), channel_id=1, source_target_pairs={{9,0},{10,1},{11,2},{12,3},{13,4},{14,5},{15,6},{25,16},{26,17},{2... | collective-permute-start | bytes 196616 | tf_op jit(solution)/shard_map/ppermute | solution.py:17
  6.5 1.3 %collective-permute-start.7 = (bf16[2,1,128,128]{3,2,0,1:T(8,128)(2,1)S(1)}, bf16[2,1,128,128]{3,2,0,1:T(8,128)(2,1)S(1)}, u32[]{:S(2)}, u32[]{:S(2)}) collective-permute-start(bf16[2,1,128,128]{3,2,0,1:T(8,128)(2,1)S(1)} %get-tuple-element.19), channel_id=1, source_target_pairs={{0,9},{1,10},{2,11},{3,12},{4,13},{5,14},{6,15},{16,25},{17,26},{1... | collective-permute-start | bytes 196616 | tf_op jit(solution)/shard_map/ppermute | solution.py:17
  7.8 1.3 %collective-permute-start.6 = (bf16[2,1,128,128]{3,2,0,1:T(8,128)(2,1)S(1)}, bf16[2,1,128,128]{3,2,0,1:T(8,128)(2,1)S(1)}, u32[]{:S(2)}, u32[]{:S(2)}) collective-permute-start(bf16[2,1,128,128]{3,2,0,1:T(8,128)(2,1)S(1)} %get-tuple-element.20), channel_id=1, source_target_pairs={{0,8},{1,9},{2,10},{3,11},{4,12},{5,13},{6,14},{7,15},{16,24},{17,... | collective-permute-start | bytes 196616 | tf_op jit(solution)/shard_map/ppermute | solution.py:17
  9.1 1.3 %collective-permute-start.5 = (bf16[2,1,128,128]{3,2,0,1:T(8,128)(2,1)S(1)}, bf16[2,1,128,128]{3,2,0,1:T(8,128)(2,1)S(1)}, u32[]{:S(2)}, u32[]{:S(2)}) collective-permute-start(bf16[2,1,128,128]{3,2,0,1:T(8,128)(2,1)S(1)} %get-tuple-element.21), channel_id=1, source_target_pairs={{0,7},{1,8},{2,9},{3,10},{4,11},{5,12},{6,13},{7,14},{8,15},{16,23... | collective-permute-start | bytes 196616 | tf_op jit(solution)/shard_map/ppermute | solution.py:17
  10.4 4.0 %collective-permute-start.4 = (bf16[2,1,128,128]{3,2,0,1:T(8,128)(2,1)S(1)}, bf16[2,1,128,128]{3,2,0,1:T(8,128)(2,1)S(1)}, u32[]{:S(2)}, u32[]{:S(2)}) collective-permute-start(bf16[2,1,128,128]{3,2,0,1:T(8,128)(2,1)S(1)} %get-tuple-element.22), channel_id=1, source_target_pairs={{0,1},{1,2},{2,3},{3,4},{4,5},{5,6},{6,7},{7,8},{8,9},{9,10},{10,1... | collective-permute-start | bytes 196616 | tf_op jit(solution)/shard_map/ppermute | solution.py:17
  14.4 0.0 copy-done.2
  14.4 0.7 copy.8
  15.1 0.0 collective-permute-done
  15.1 4.9 %collective-permute-start.1 = (bf16[2,1,128,128]{3,2,0,1:T(8,128)(2,1)S(1)}, bf16[2,1,128,128]{3,2,0,1:T(8,128)(2,1)S(1)}, u32[]{:S(2)}, u32[]{:S(2)}) collective-permute-start(bf16[2,1,128,128]{3,2,0,1:T(8,128)(2,1)S(1)} %get-tuple-element.25), channel_id=1, source_target_pairs={{8,0},{9,1},{10,2},{11,3},{12,4},{13,5},{14,6},{15,7},{24,16},{25,... | collective-permute-start | bytes 196616 | tf_op jit(solution)/shard_map/ppermute | solution.py:17
  20.0 1.3 %collective-permute-done.1 = bf16[2,1,128,128]{3,2,0,1:T(8,128)(2,1)S(1)} collective-permute-done((bf16[2,1,128,128]{3,2,0,1:T(8,128)(2,1)S(1)}, bf16[2,1,128,128]{3,2,0,1:T(8,128)(2,1)S(1)}, u32[]{:S(2)}, u32[]{:S(2)}) %collective-permute-start.1) | collective-permute-done | bytes 65568 | tf_op jit(solution)/shard_map/ppermute | solution.py:17
  21.3 5.4 %collective-permute-start.2 = (bf16[2,1,128,128]{3,2,0,1:T(8,128)(2,1)S(1)}, bf16[2,1,128,128]{3,2,0,1:T(8,128)(2,1)S(1)}, u32[]{:S(2)}, u32[]{:S(2)}) collective-permute-start(bf16[2,1,128,128]{3,2,0,1:T(8,128)(2,1)S(1)} %get-tuple-element.24), channel_id=1, source_target_pairs={{7,0},{8,1},{9,2},{10,3},{11,4},{12,5},{13,6},{14,7},{15,8},{23,16... | collective-permute-start | bytes 196616 | tf_op jit(solution)/shard_map/ppermute | solution.py:17
  26.8 1.3 %collective-permute-done.2 = bf16[2,1,128,128]{3,2,0,1:T(8,128)(2,1)S(1)} collective-permute-done((bf16[2,1,128,128]{3,2,0,1:T(8,128)(2,1)S(1)}, bf16[2,1,128,128]{3,2,0,1:T(8,128)(2,1)S(1)}, u32[]{:S(2)}, u32[]{:S(2)}) %collective-permute-start.2) | collective-permute-done | bytes 65568 | tf_op jit(solution)/shard_map/ppermute | solution.py:17
  28.1 2.2 %collective-permute-start.3 = (bf16[2,1,128,128]{3,2,0,1:T(8,128)(2,1)S(1)}, bf16[2,1,128,128]{3,2,0,1:T(8,128)(2,1)S(1)}, u32[]{:S(2)}, u32[]{:S(2)}) collective-permute-start(bf16[2,1,128,128]{3,2,0,1:T(8,128)(2,1)S(1)} %get-tuple-element.23), channel_id=1, source_target_pairs={{1,0},{2,1},{3,2},{4,3},{5,4},{6,5},{7,6},{8,7},{9,8},{10,9},{11,1... | collective-permute-start | bytes 196616 | tf_op jit(solution)/shard_map/ppermute | solution.py:17
  30.3 3.7 %collective-permute-done.3 = bf16[2,1,128,128]{3,2,0,1:T(8,128)(2,1)S(1)} collective-permute-done((bf16[2,1,128,128]{3,2,0,1:T(8,128)(2,1)S(1)}, bf16[2,1,128,128]{3,2,0,1:T(8,128)(2,1)S(1)}, u32[]{:S(2)}, u32[]{:S(2)}) %collective-permute-start.3) | collective-permute-done | bytes 65568 | tf_op jit(solution)/shard_map/ppermute | solution.py:17
  34.0 0.0 collective-permute-done.4
  34.0 0.0 collective-permute-done.5
  34.1 0.0 collective-permute-done.6
  34.1 0.0 collective-permute-done.7
  34.1 0.0 copy-start.1
  34.1 0.8 copy-done.1
  34.9 7.6 %shard_map.74.refs_0_.own = bf16[24,128,128]{2,1,0:T(8,128)(2,1)} custom-call(s32[27,24]{1,0:T(8,128)} %bitcast.101, bf16[24,128,128]{2,1,0:T(8,128)(2,1)} %bitcast.95, bf16[16,128,128]{2,1,0:T(8,128)(2,1)} %bitcast.98, bf16[27,128,128]{2,1,0:T(8,128)(2,1)} %bitcast.96), custom_call_target="tpu_custom_call" | custom-call | tf_op jit(solution)/shard_map/pallas_call | solution.py:118
  42.5 1.3 %collective-permute-start.8 = (bf16[24,128,128]{2,1,0:T(8,128)(2,1)}, bf16[24,128,128]{2,1,0:T(8,128)(2,1)S(1)}, u32[]{:S(2)}, u32[]{:S(2)}) collective-permute-start(bf16[24,128,128]{2,1,0:T(8,128)(2,1)} %shard_map.74.refs_0_.own), channel_id=1, source_target_pairs={{0,16},{1,17},{2,18},{3,19},{4,20},{5,21},{6,22},{7,23},{8,24},{9,... | collective-permute-start | bytes 2359304 | tf_op jit(solution)/shard_map/ppermute | solution.py:17
  43.8 6.6 %collective-permute-done.8.refs_1_.skip = bf16[24,128,128]{2,1,0:T(8,128)(2,1)S(1)} collective-permute-done((bf16[24,128,128]{2,1,0:T(8,128)(2,1)}, bf16[24,128,128]{2,1,0:T(8,128)(2,1)S(1)}, u32[]{:S(2)}, u32[]{:S(2)}) %collective-permute-start.8) | collective-permute-done | bytes 786464 | tf_op jit(solution)/shard_map/ppermute | solution.py:17
  50.4 0.0 copy-start
  50.4 0.9 copy-done
  51.3 2.6 %shard_map.75 = (bf16[8,2,128,128]{3,2,1,0:T(8,128)(2,1)}, bf16[8,2,128,128]{3,2,1,0:T(8,128)(2,1)}) custom-call(s32[8,2]{1,0:T(8,128)} %copy.9.rows, s32[8]{0:T(128)} %bitcast.104, bf16[24,128,128]{2,1,0:T(8,128)(2,1)} %shard_map.74.refs_0_.own, bf16[24,128,128]{2,1,0:T(8,128)(2,1)} %copy-done), custom_call_target="tpu_custom_call" | custom-call | tf_op jit(solution)/shard_map/pallas_call | solution.py:95
  53.9 1.3 %fusion.7 = (bf16[2,2,128,128]{3,2,0,1:T(8,128)(2,1)S(1)}, bf16[2,2,128,128]{3,2,0,1:T(8,128)(2,1)S(1)}, bf16[2,2,128,128]{3,2,0,1:T(8,128)(2,1)S(1)}, bf16[2,2,...) fusion(bf16[8,2,1,128,128]{4,3,1,0,2:T(8,128)(2,1)} %bitcast.10, ...), kind=kLoop, calls=%fused_computation.24 | loop fusion | flops 524288 | bytes 2097152 | tf_op jit(solution)/shard_map/squeeze | solution.py:105
  55.3 5.7 %collective-permute-start.9 = (bf16[2,2,128,128]{3,2,0,1:T(8,128)(2,1)S(1)}, bf16[2,2,128,128]{3,2,0,1:T(8,128)(2,1)S(1)}, u32[]{:S(2)}, u32[]{:S(2)}) collective-permute-start(bf16[2,2,128,128]{3,2,0,1:T(8,128)(2,1)S(1)} %get-tuple-element.12), channel_id=1, source_target_pairs={{9,0},{10,1},{11,2},{12,3},{13,4},{14,5},{15,6},{25,16},{26,17},{2... | collective-permute-start | bytes 393224 | tf_op jit(solution)/shard_map/ppermute | solution.py:17
  61.0 1.3 %collective-permute-start.16 = (bf16[2,2,128,128]{3,2,0,1:T(8,128)(2,1)S(1)}, bf16[2,2,128,128]{3,2,0,1:T(8,128)(2,1)S(1)}, u32[]{:S(2)}, u32[]{:S(2)}) collective-permute-start(bf16[2,2,128,128]{3,2,0,1:T(8,128)(2,1)S(1)} %get-tuple-element.11), channel_id=1, source_target_pairs={{0,9},{1,10},{2,11},{3,12},{4,13},{5,14},{6,15},{16,25},{17,26},{1... | collective-permute-start | bytes 393224 | tf_op jit(solution)/shard_map/ppermute | solution.py:17
  62.3 5.9 %collective-permute-start.10 = (bf16[2,2,128,128]{3,2,0,1:T(8,128)(2,1)S(1)}, bf16[2,2,128,128]{3,2,0,1:T(8,128)(2,1)S(1)}, u32[]{:S(2)}, u32[]{:S(2)}) collective-permute-start(bf16[2,2,128,128]{3,2,0,1:T(8,128)(2,1)S(1)} %get-tuple-element.13), channel_id=1, source_target_pairs={{8,0},{9,1},{10,2},{11,3},{12,4},{13,5},{14,6},{15,7},{24,16},{25,... | collective-permute-start | bytes 393224 | tf_op jit(solution)/shard_map/ppermute | solution.py:17
  68.2 1.3 %collective-permute-start.11 = (bf16[2,2,128,128]{3,2,0,1:T(8,128)(2,1)S(1)}, bf16[2,2,128,128]{3,2,0,1:T(8,128)(2,1)S(1)}, u32[]{:S(2)}, u32[]{:S(2)}) collective-permute-start(bf16[2,2,128,128]{3,2,0,1:T(8,128)(2,1)S(1)} %get-tuple-element.14), channel_id=1, source_target_pairs={{7,0},{8,1},{9,2},{10,3},{11,4},{12,5},{13,6},{14,7},{15,8},{23,16... | collective-permute-start | bytes 393224 | tf_op jit(solution)/shard_map/ppermute | solution.py:17
  69.5 3.1 %collective-permute-start.12 = (bf16[2,2,128,128]{3,2,0,1:T(8,128)(2,1)S(1)}, bf16[2,2,128,128]{3,2,0,1:T(8,128)(2,1)S(1)}, u32[]{:S(2)}, u32[]{:S(2)}) collective-permute-start(bf16[2,2,128,128]{3,2,0,1:T(8,128)(2,1)S(1)} %get-tuple-element.15), channel_id=1, source_target_pairs={{1,0},{2,1},{3,2},{4,3},{5,4},{6,5},{7,6},{8,7},{9,8},{10,9},{11,1... | collective-permute-start | bytes 393224 | tf_op jit(solution)/shard_map/ppermute | solution.py:17
  72.6 0.0 collective-permute-done.9
  72.6 3.1 %collective-permute-start.13 = (bf16[2,2,128,128]{3,2,0,1:T(8,128)(2,1)S(1)}, bf16[2,2,128,128]{3,2,0,1:T(8,128)(2,1)S(1)}, u32[]{:S(2)}, u32[]{:S(2)}) collective-permute-start(bf16[2,2,128,128]{3,2,0,1:T(8,128)(2,1)S(1)} %get-tuple-element.16), channel_id=1, source_target_pairs={{0,1},{1,2},{2,3},{3,4},{4,5},{5,6},{6,7},{7,8},{8,9},{9,10},{10,1... | collective-permute-start | bytes 393224 | tf_op jit(solution)/shard_map/ppermute | solution.py:17
  75.7 0.0 collective-permute-done.10
  75.7 1.3 %collective-permute-start.14 = (bf16[2,2,128,128]{3,2,0,1:T(8,128)(2,1)S(1)}, bf16[2,2,128,128]{3,2,0,1:T(8,128)(2,1)S(1)}, u32[]{:S(2)}, u32[]{:S(2)}) collective-permute-start(bf16[2,2,128,128]{3,2,0,1:T(8,128)(2,1)S(1)} %get-tuple-element.17), channel_id=1, source_target_pairs={{0,7},{1,8},{2,9},{3,10},{4,11},{5,12},{6,13},{7,14},{8,15},{16,23... | collective-permute-start | bytes 393224 | tf_op jit(solution)/shard_map/ppermute | solution.py:17
  77.1 0.0 collective-permute-done.11
  77.1 1.3 %collective-permute-start.15 = (bf16[2,2,128,128]{3,2,0,1:T(8,128)(2,1)S(1)}, bf16[2,2,128,128]{3,2,0,1:T(8,128)(2,1)S(1)}, u32[]{:S(2)}, u32[]{:S(2)}) collective-permute-start(bf16[2,2,128,128]{3,2,0,1:T(8,128)(2,1)S(1)} %get-tuple-element.18), channel_id=1, source_target_pairs={{0,8},{1,9},{2,10},{3,11},{4,12},{5,13},{6,14},{7,15},{16,24},{17,... | collective-permute-start | bytes 393224 | tf_op jit(solution)/shard_map/ppermute | solution.py:17
  78.4 0.0 collective-permute-done.12
  78.4 7.5 %collective-permute-done.13 = bf16[2,2,128,128]{3,2,0,1:T(8,128)(2,1)S(1)} collective-permute-done((bf16[2,2,128,128]{3,2,0,1:T(8,128)(2,1)S(1)}, bf16[2,2,128,128]{3,2,0,1:T(8,128)(2,1)S(1)}, u32[]{:S(2)}, u32[]{:S(2)}) %collective-permute-start.13) | collective-permute-done | bytes 131104 | tf_op jit(solution)/shard_map/ppermute | solution.py:17
  86.0 0.0 collective-permute-done.14
  86.0 8.7 %collective-permute-done.15 = bf16[2,2,128,128]{3,2,0,1:T(8,128)(2,1)S(1)} collective-permute-done((bf16[2,2,128,128]{3,2,0,1:T(8,128)(2,1)S(1)}, bf16[2,2,128,128]{3,2,0,1:T(8,128)(2,1)S(1)}, u32[]{:S(2)}, u32[]{:S(2)}) %collective-permute-start.15) | collective-permute-done | bytes 131104 | tf_op jit(solution)/shard_map/ppermute | solution.py:17
  94.7 0.0 collective-permute-done.16
  94.7 0.1 copy.18
  94.8 1.1 slice_bitcast_fusion
  95.9 10.9 %shard_map.76 = bf16[24,128,128]{2,1,0:T(8,128)(2,1)} custom-call(s32[27,24]{1,0:T(8,128)} %bitcast.102, bf16[24,128,128]{2,1,0:T(8,128)(2,1)} %shard_map.74.refs_0_.own, bf16[16,128,128]{2,1,0:T(8,128)(2,1)} %get-tuple-element.10.arrived, bf16[24,128,128]{2,1,0:T(8,128)(2,1)} %copy-done, bf16[16,128,128]{2,1,0:T(8,128)(2,1)} %get-tuple-element.9.skip_arrived, ...), custom_call_target="tpu_custom_call" | custom-call | tf_op jit(solution)/shard_map/pallas_call | solution.py:127
  (16 shorter events, 0.3 us)
Async XLA Ops:
  0.0 0.7 copy-start.3
  3.4 11.0 %copy-start.2 = (s32[1,27,24]{1,2,0:T(8,128)S(1)}, s32[1,27,24]{1,2,0:T(8,128)}, u32[]{:S(2)}) copy-start(s32[1,27,24]{1,2,0:T(8,128)} %param.13) | copy-start | bytes 7780
  4.5 10.6 %collective-permute-start = (bf16[2,1,128,128]{3,2,0,1:T(8,128)(2,1)S(1)}, bf16[2,1,128,128]{3,2,0,1:T(8,128)(2,1)S(1)}, u32[]{:S(2)}, u32[]{:S(2)}) collective-permute-start(bf16[2,1,128,128]{3,2,0,1:T(8,128)(2,1)S(1)} %get-tuple-element.26), channel_id=1, source_target_pairs={{9,0},{10,1},{11,2},{12,3},{13,4},{14,5},{15,6},{25,16},{26,17},{2... | collective-permute-start | bytes 196616 | tf_op jit(solution)/shard_map/ppermute | solution.py:17
  6.5 27.6 %collective-permute-start.7 = (bf16[2,1,128,128]{3,2,0,1:T(8,128)(2,1)S(1)}, bf16[2,1,128,128]{3,2,0,1:T(8,128)(2,1)S(1)}, u32[]{:S(2)}, u32[]{:S(2)}) collective-permute-start(bf16[2,1,128,128]{3,2,0,1:T(8,128)(2,1)S(1)} %get-tuple-element.19), channel_id=1, source_target_pairs={{0,9},{1,10},{2,11},{3,12},{4,13},{5,14},{6,15},{16,25},{17,26},{1... | collective-permute-start | bytes 196616 | tf_op jit(solution)/shard_map/ppermute | solution.py:17
  7.8 26.3 %collective-permute-start.6 = (bf16[2,1,128,128]{3,2,0,1:T(8,128)(2,1)S(1)}, bf16[2,1,128,128]{3,2,0,1:T(8,128)(2,1)S(1)}, u32[]{:S(2)}, u32[]{:S(2)}) collective-permute-start(bf16[2,1,128,128]{3,2,0,1:T(8,128)(2,1)S(1)} %get-tuple-element.20), channel_id=1, source_target_pairs={{0,8},{1,9},{2,10},{3,11},{4,12},{5,13},{6,14},{7,15},{16,24},{17,... | collective-permute-start | bytes 196616 | tf_op jit(solution)/shard_map/ppermute | solution.py:17
  9.1 25.0 %collective-permute-start.5 = (bf16[2,1,128,128]{3,2,0,1:T(8,128)(2,1)S(1)}, bf16[2,1,128,128]{3,2,0,1:T(8,128)(2,1)S(1)}, u32[]{:S(2)}, u32[]{:S(2)}) collective-permute-start(bf16[2,1,128,128]{3,2,0,1:T(8,128)(2,1)S(1)} %get-tuple-element.21), channel_id=1, source_target_pairs={{0,7},{1,8},{2,9},{3,10},{4,11},{5,12},{6,13},{7,14},{8,15},{16,23... | collective-permute-start | bytes 196616 | tf_op jit(solution)/shard_map/ppermute | solution.py:17
  10.4 23.6 %collective-permute-start.4 = (bf16[2,1,128,128]{3,2,0,1:T(8,128)(2,1)S(1)}, bf16[2,1,128,128]{3,2,0,1:T(8,128)(2,1)S(1)}, u32[]{:S(2)}, u32[]{:S(2)}) collective-permute-start(bf16[2,1,128,128]{3,2,0,1:T(8,128)(2,1)S(1)} %get-tuple-element.22), channel_id=1, source_target_pairs={{0,1},{1,2},{2,3},{3,4},{4,5},{5,6},{6,7},{7,8},{8,9},{9,10},{10,1... | collective-permute-start | bytes 196616 | tf_op jit(solution)/shard_map/ppermute | solution.py:17
  15.1 6.2 %collective-permute-start.1 = (bf16[2,1,128,128]{3,2,0,1:T(8,128)(2,1)S(1)}, bf16[2,1,128,128]{3,2,0,1:T(8,128)(2,1)S(1)}, u32[]{:S(2)}, u32[]{:S(2)}) collective-permute-start(bf16[2,1,128,128]{3,2,0,1:T(8,128)(2,1)S(1)} %get-tuple-element.25), channel_id=1, source_target_pairs={{8,0},{9,1},{10,2},{11,3},{12,4},{13,5},{14,6},{15,7},{24,16},{25,... | collective-permute-start | bytes 196616 | tf_op jit(solution)/shard_map/ppermute | solution.py:17
  21.3 6.8 %collective-permute-start.2 = (bf16[2,1,128,128]{3,2,0,1:T(8,128)(2,1)S(1)}, bf16[2,1,128,128]{3,2,0,1:T(8,128)(2,1)S(1)}, u32[]{:S(2)}, u32[]{:S(2)}) collective-permute-start(bf16[2,1,128,128]{3,2,0,1:T(8,128)(2,1)S(1)} %get-tuple-element.24), channel_id=1, source_target_pairs={{7,0},{8,1},{9,2},{10,3},{11,4},{12,5},{13,6},{14,7},{15,8},{23,16... | collective-permute-start | bytes 196616 | tf_op jit(solution)/shard_map/ppermute | solution.py:17
  28.1 5.9 %collective-permute-start.3 = (bf16[2,1,128,128]{3,2,0,1:T(8,128)(2,1)S(1)}, bf16[2,1,128,128]{3,2,0,1:T(8,128)(2,1)S(1)}, u32[]{:S(2)}, u32[]{:S(2)}) collective-permute-start(bf16[2,1,128,128]{3,2,0,1:T(8,128)(2,1)S(1)} %get-tuple-element.23), channel_id=1, source_target_pairs={{1,0},{2,1},{3,2},{4,3},{5,4},{6,5},{7,6},{8,7},{9,8},{10,9},{11,1... | collective-permute-start | bytes 196616 | tf_op jit(solution)/shard_map/ppermute | solution.py:17
  34.1 0.8 copy-start.1
  42.5 7.9 %collective-permute-start.8 = (bf16[24,128,128]{2,1,0:T(8,128)(2,1)}, bf16[24,128,128]{2,1,0:T(8,128)(2,1)S(1)}, u32[]{:S(2)}, u32[]{:S(2)}) collective-permute-start(bf16[24,128,128]{2,1,0:T(8,128)(2,1)} %shard_map.74.refs_0_.own), channel_id=1, source_target_pairs={{0,16},{1,17},{2,18},{3,19},{4,20},{5,21},{6,22},{7,23},{8,24},{9,... | collective-permute-start | bytes 2359304 | tf_op jit(solution)/shard_map/ppermute | solution.py:17
  50.4 0.9 copy-start
  55.3 17.3 %collective-permute-start.9 = (bf16[2,2,128,128]{3,2,0,1:T(8,128)(2,1)S(1)}, bf16[2,2,128,128]{3,2,0,1:T(8,128)(2,1)S(1)}, u32[]{:S(2)}, u32[]{:S(2)}) collective-permute-start(bf16[2,2,128,128]{3,2,0,1:T(8,128)(2,1)S(1)} %get-tuple-element.12), channel_id=1, source_target_pairs={{9,0},{10,1},{11,2},{12,3},{13,4},{14,5},{15,6},{25,16},{26,17},{2... | collective-permute-start | bytes 393224 | tf_op jit(solution)/shard_map/ppermute | solution.py:17
  61.0 33.7 %collective-permute-start.16 = (bf16[2,2,128,128]{3,2,0,1:T(8,128)(2,1)S(1)}, bf16[2,2,128,128]{3,2,0,1:T(8,128)(2,1)S(1)}, u32[]{:S(2)}, u32[]{:S(2)}) collective-permute-start(bf16[2,2,128,128]{3,2,0,1:T(8,128)(2,1)S(1)} %get-tuple-element.11), channel_id=1, source_target_pairs={{0,9},{1,10},{2,11},{3,12},{4,13},{5,14},{6,15},{16,25},{17,26},{1... | collective-permute-start | bytes 393224 | tf_op jit(solution)/shard_map/ppermute | solution.py:17
  62.3 13.4 %collective-permute-start.10 = (bf16[2,2,128,128]{3,2,0,1:T(8,128)(2,1)S(1)}, bf16[2,2,128,128]{3,2,0,1:T(8,128)(2,1)S(1)}, u32[]{:S(2)}, u32[]{:S(2)}) collective-permute-start(bf16[2,2,128,128]{3,2,0,1:T(8,128)(2,1)S(1)} %get-tuple-element.13), channel_id=1, source_target_pairs={{8,0},{9,1},{10,2},{11,3},{12,4},{13,5},{14,6},{15,7},{24,16},{25,... | collective-permute-start | bytes 393224 | tf_op jit(solution)/shard_map/ppermute | solution.py:17
  68.2 8.9 %collective-permute-start.11 = (bf16[2,2,128,128]{3,2,0,1:T(8,128)(2,1)S(1)}, bf16[2,2,128,128]{3,2,0,1:T(8,128)(2,1)S(1)}, u32[]{:S(2)}, u32[]{:S(2)}) collective-permute-start(bf16[2,2,128,128]{3,2,0,1:T(8,128)(2,1)S(1)} %get-tuple-element.14), channel_id=1, source_target_pairs={{7,0},{8,1},{9,2},{10,3},{11,4},{12,5},{13,6},{14,7},{15,8},{23,16... | collective-permute-start | bytes 393224 | tf_op jit(solution)/shard_map/ppermute | solution.py:17
  69.5 8.9 %collective-permute-start.12 = (bf16[2,2,128,128]{3,2,0,1:T(8,128)(2,1)S(1)}, bf16[2,2,128,128]{3,2,0,1:T(8,128)(2,1)S(1)}, u32[]{:S(2)}, u32[]{:S(2)}) collective-permute-start(bf16[2,2,128,128]{3,2,0,1:T(8,128)(2,1)S(1)} %get-tuple-element.15), channel_id=1, source_target_pairs={{1,0},{2,1},{3,2},{4,3},{5,4},{6,5},{7,6},{8,7},{9,8},{10,9},{11,1... | collective-permute-start | bytes 393224 | tf_op jit(solution)/shard_map/ppermute | solution.py:17
  72.6 13.3 %collective-permute-start.13 = (bf16[2,2,128,128]{3,2,0,1:T(8,128)(2,1)S(1)}, bf16[2,2,128,128]{3,2,0,1:T(8,128)(2,1)S(1)}, u32[]{:S(2)}, u32[]{:S(2)}) collective-permute-start(bf16[2,2,128,128]{3,2,0,1:T(8,128)(2,1)S(1)} %get-tuple-element.16), channel_id=1, source_target_pairs={{0,1},{1,2},{2,3},{3,4},{4,5},{5,6},{6,7},{7,8},{8,9},{9,10},{10,1... | collective-permute-start | bytes 393224 | tf_op jit(solution)/shard_map/ppermute | solution.py:17
  75.7 10.2 %collective-permute-start.14 = (bf16[2,2,128,128]{3,2,0,1:T(8,128)(2,1)S(1)}, bf16[2,2,128,128]{3,2,0,1:T(8,128)(2,1)S(1)}, u32[]{:S(2)}, u32[]{:S(2)}) collective-permute-start(bf16[2,2,128,128]{3,2,0,1:T(8,128)(2,1)S(1)} %get-tuple-element.17), channel_id=1, source_target_pairs={{0,7},{1,8},{2,9},{3,10},{4,11},{5,12},{6,13},{7,14},{8,15},{16,23... | collective-permute-start | bytes 393224 | tf_op jit(solution)/shard_map/ppermute | solution.py:17
  77.1 17.6 %collective-permute-start.15 = (bf16[2,2,128,128]{3,2,0,1:T(8,128)(2,1)S(1)}, bf16[2,2,128,128]{3,2,0,1:T(8,128)(2,1)S(1)}, u32[]{:S(2)}, u32[]{:S(2)}) collective-permute-start(bf16[2,2,128,128]{3,2,0,1:T(8,128)(2,1)S(1)} %get-tuple-element.18), channel_id=1, source_target_pairs={{0,8},{1,9},{2,10},{3,11},{4,12},{5,13},{6,14},{7,15},{16,24},{17,... | collective-permute-start | bytes 393224 | tf_op jit(solution)/shard_map/ppermute | solution.py:17

commit v2 on v1

v2 whole, which is shorter than its diff:
```python
import jax
import jax.numpy as jnp
from jax import lax
from jax.experimental import pallas as pl
from jax.experimental.pallas import tpu as pltpu
from jax.sharding import PartitionSpec as P

GRID_B = 8

step_rows = (-1, -1, -1, 0, 0, 1, 1, 1)
step_cols = (-1, 0, 1, -1, 1, -1, 0, 1)


def conv_tiles(ids, pairs, emit, tiles, koff):
    def body(step, _):
        t = step * 2
        terms = [(w, table, k) for k in range(koff) for w, table in pairs]
        acc = None
        for i in range(0, len(terms), 2):
            lhs, rhs = [], []
            for w, table, k in terms[i : i + 2]:
                lhs.append(w[k])
                rhs.append(jnp.concatenate([table[ids[k, t]], table[ids[k, t + 1]]], axis=1))
            part = jnp.dot(
                jnp.concatenate(lhs, axis=1),
                jnp.concatenate(rhs, axis=0),
                preferred_element_type=jnp.float32,
            )
            acc = part if acc is None else acc + part
        emit(t, acc)
        return 0

    lax.fori_loop(0, tiles // 2, body, 0)


MESH = pl.DeviceIdType.MESH


def network(
    ids, rows, counts, feats, w1_hbm, w2_hbm, w3_hbm, out,
    table1, table2, table3, w1, w2, w3, acc,
    outbox1, outbox2, outbox3, inbox1, inbox2, inbox3,
    local_sems, send1, recv1, send2, recv2, send3, recv3, send_skip, recv_skip,
):
    tiles, _, vox = feats.shape
    dirs, cap = rows.shape
    koff = w1.shape[0]
    section = lax.axis_index("section")
    me = lax.axis_index("space")
    grid_a = lax.axis_size("space") // GRID_B
    row, col = me // GRID_B, me % GRID_B

    def inside(d, sign):
        r, c = row + sign * step_rows[d], col + sign * step_cols[d]
        return (r >= 0) & (r < grid_a) & (c >= 0) & (c < GRID_B)

    def target(d):
        return {"section": section, "space": me + step_rows[d] * GRID_B + step_cols[d]}

    sibling = {"section": 1 - section, "space": me}

    loads = [
        pltpu.make_async_copy(src, dst, local_sems.at[i])
        for i, (src, dst) in enumerate(
            [(feats, table1.at[pl.ds(0, tiles)]), (w1_hbm, w1), (w2_hbm, w2), (w3_hbm, w3)]
        )
    ]
    for load in loads:
        load.start()

    barrier = pltpu.get_barrier_semaphore()
    for d in range(dirs):

        @pl.when(inside(d, 1))
        def _():
            pl.semaphore_signal(barrier, inc=1, device_id=target(d), device_id_type=MESH)

    pl.semaphore_signal(barrier, inc=1, device_id=sibling, device_id_type=MESH)
    peers = jnp.int32(1)
    for d in range(dirs):
        peers += jnp.where(inside(d, -1), 1, 0).astype(jnp.int32)
    pl.semaphore_wait(barrier, peers)

    def halo_copy(d, outbox, inbox, send, recv):
        return pltpu.make_async_remote_copy(
            src_ref=outbox.at[d],
            dst_ref=inbox.at[d],
            send_sem=send.at[d],
            recv_sem=recv.at[d],
            device_id=target(d),
            device_id_type=MESH,
        )

    def halo_send(table, outbox, inbox, send, recv):
        for d in range(dirs):
            for j in range(cap):
                tile = table[rows[d, j]]
                outbox[d, j] = jnp.where(j < counts[d], tile, jnp.zeros_like(tile))

            @pl.when(inside(d, 1))
            def _():
                halo_copy(d, outbox, inbox, send, recv).start()

    def halo_receive(table, outbox, inbox, send, recv):
        for d in range(dirs):
            place = pl.ds(tiles + d * cap, cap)

            @pl.when(inside(d, -1))
            def _():
                halo_copy(d, outbox, inbox, send, recv).wait_recv()
                table[place] = inbox[d]

            @pl.when(jnp.logical_not(inside(d, -1)))
            def _():
                table[place] = jnp.zeros((cap,) + table.shape[1:], table.dtype)

        table[tiles + dirs * cap] = jnp.zeros(table.shape[1:], table.dtype)

    def halo_sent(outbox, inbox, send, recv):
        for d in range(dirs):

            @pl.when(inside(d, 1))
            def _():
                halo_copy(d, outbox, inbox, send, recv).wait_send()

    def skip_copy(t):
        return pltpu.make_async_remote_copy(
            src_ref=table2.at[pl.ds(t, 2)],
            dst_ref=table3.at[pl.ds(t, 2)],
            send_sem=send_skip.at[t // 2],
            recv_sem=recv_skip.at[t // 2],
            device_id=sibling,
            device_id_type=MESH,
        )

    halo1 = (outbox1, inbox1, send1, recv1)
    halo2 = (outbox2, inbox2, send2, recv2)
    halo3 = (outbox3, inbox3, send3, recv3)

    loads[0].wait()
    halo_send(table1, *halo1)
    halo_receive(table1, *halo1)
    loads[1].wait()

    def emit_first(t, part):
        part = jnp.maximum(part, 0.0).astype(table2.dtype)
        table2[t] = part[:, :vox]
        table2[t + 1] = part[:, vox:]

        @pl.when(section == 0)
        def _():
            skip_copy(t).start()

    conv_tiles(ids, [(w1, table1)], emit_first, tiles, koff)
    halo_send(table2, *halo2)

    @pl.when(section == 1)
    def _():
        lax.fori_loop(0, tiles // 2, lambda i, _: (skip_copy(2 * i).wait_recv(), 0)[1], 0)
        halo_send(table3, *halo3)

    halo_receive(table2, *halo2)
    loads[2].wait()
    loads[3].wait()

    def emit_out(t, part):
        acc[t // 2] = part
        part = jnp.maximum(part, 0.0).astype(out.dtype)
        out[t] = part[:, :vox]
        out[t + 1] = part[:, vox:]

    conv_tiles(ids, [(w2, table2)], emit_out, tiles, koff)

    @pl.when(section == 0)
    def _():
        lax.fori_loop(0, tiles // 2, lambda i, _: (skip_copy(2 * i).wait_send(), 0)[1], 0)

    @pl.when(section == 1)
    def _():
        halo_receive(table3, *halo3)

        def emit_sum(t, part):
            part = jnp.maximum(part + acc[t // 2], 0.0).astype(out.dtype)
            out[t] = part[:, :vox]
            out[t + 1] = part[:, vox:]

        conv_tiles(ids, [(w3, table3)], emit_sum, tiles, koff)
        halo_sent(*halo3)

    halo_sent(*halo1)
    halo_sent(*halo2)


def local(feats, w_first, w_second, w_skip, send_tiles, send_counts, neighbours):
    ids, send_rows, counts = neighbours[0], send_tiles[0], send_counts[0]
    own = feats[0]
    tiles, channels, vox = own.shape
    dirs, cap = send_rows.shape
    table = pltpu.VMEM((tiles + dirs * cap + 1, channels, vox), own.dtype)
    weights = pltpu.VMEM(w_skip.shape, w_skip.dtype)
    box = pltpu.VMEM((dirs, cap, channels, vox), own.dtype)
    smem = pl.BlockSpec(memory_space=pltpu.SMEM)
    anywhere = pl.BlockSpec(memory_space=pl.ANY)
    second = pl.pallas_call(
        network,
        out_shape=jax.ShapeDtypeStruct((tiles, channels, vox), own.dtype),
        in_specs=[smem] * 3 + [anywhere] * 4,
        out_specs=pl.BlockSpec(memory_space=pltpu.VMEM),
        scratch_shapes=[table] * 3
        + [weights] * 3
        + [pltpu.VMEM((tiles // 2, channels, 2 * vox), jnp.float32)]
        + [box] * 6
        + [pltpu.SemaphoreType.DMA((4,))]
        + [pltpu.SemaphoreType.DMA((dirs,))] * 6
        + [pltpu.SemaphoreType.DMA((tiles // 2,))] * 2,
        compiler_params=pltpu.CompilerParams(
            collective_id=0, has_side_effects=True, vmem_limit_bytes=40 * 2**20
        ),
    )(ids, send_rows, counts, own, w_first[0], w_second[0], w_skip)
    return second[None]


def solution(mesh):
    placed = (
        P("section", "space", None, None),
        P("section", None, None, None),
        P("section", None, None, None),
        P(),
        P("section", "space", None),
        P("section", "space"),
        P("section", None, "space"),
    )
    return jax.shard_map(
        local,
        mesh=mesh,
        in_specs=placed,
        out_specs=P("section", "space", None, None),
        check_vma=False,
    )
```

time: 107 us -> 46.3 us (0.43)
  the two profiles are of different devices: /device:TPU:27 before, /device:TPU:31 now
where the time goes in v2:
time: 46.3 us; the launch traced here: 45.9 us
  Pallas kernels  38.9 us (84%)
  local copies, waits for them, and re-layouts  7.03 us (15%)
    pallas_call x1, Pallas kernels, local(): pl.pallas_call(network, out_shape=jax.ShapeDtypeStruct((tiles, channels,...  38.9 us
    unnamed x14, local copies, waits for them, and re-layouts  6.26 us

profile of v2, /device:TPU:31, one launch (start us, length us, event | category | flops | bytes accessed | tf_op | source)
XLA Modules:
  0.0 45.9 jit_solution(5759619122382277795)
XLA Ops:
  0.0 0.0 copy-start.5
  0.0 0.8 %copy.9.rows = s32[8,2]{1,0:T(8,128)S(1)} copy(s32[8,2]{0,1:T(2,128)} %bitcast.13) | data formatting | bytes 128 | tf_op jit(solution)/shard_map/squeeze | solution.py:195
  0.8 0.0 copy-done.5
  0.8 0.1 copy.8
  0.9 0.0 copy-start.4
  0.9 0.7 %copy-done.4 = s32[1,8]{1,0:T(1,128)S(1)} copy-done((s32[1,8]{1,0:T(1,128)S(1)}, s32[1,8]{1,0:T(1,128)}, u32[]{:S(2)}) %copy-start.4) | copy-done | bytes 56
  1.5 0.0 copy-start
  1.5 1.2 %copy-done = bf16[1,27,128,128]{3,2,1,0:T(8,128)(2,1)S(1)} copy-done((bf16[1,27,128,128]{3,2,1,0:T(8,128)(2,1)S(1)}, bf16[1,27,128,128]{3,2,1,0:T(8,128)(2,1)}, u32[]{:S(2)}) %copy-start) | copy-done | bytes 884760
  2.7 0.0 copy-start.1
  2.7 1.2 %copy-done.1 = bf16[1,27,128,128]{3,2,1,0:T(8,128)(2,1)S(1)} copy-done((bf16[1,27,128,128]{3,2,1,0:T(8,128)(2,1)S(1)}, bf16[1,27,128,128]{3,2,1,0:T(8,128)(2,1)}, u32[]{:S(2)}) %copy-start.1) | copy-done | bytes 884760
  3.9 0.0 copy-start.2
  3.9 1.2 %copy-done.2 = bf16[27,128,128]{2,1,0:T(8,128)(2,1)S(1)} copy-done((bf16[27,128,128]{2,1,0:T(8,128)(2,1)S(1)}, bf16[27,128,128]{2,1,0:T(8,128)(2,1)}, u32[]{:S(2)}) %copy-start.2) | copy-done | bytes 884760
  5.0 0.0 copy-start.3
  5.0 1.1 %copy-done.3 = bf16[1,24,128,128]{3,2,1,0:T(8,128)(2,1)S(1)} copy-done((bf16[1,24,128,128]{3,2,1,0:T(8,128)(2,1)S(1)}, bf16[1,24,128,128]{3,2,1,0:T(8,128)(2,1)}, u32[]{:S(2)}) %copy-start.3) | copy-done | bytes 786456
  6.2 38.9 %shard_map.73 = bf16[24,128,128]{2,1,0:T(8,128)(2,1)S(1)} custom-call(s32[27,24]{1,0:T(8,128)S(1)} %bitcast.11, s32[8,2]{1,0:T(8,128)S(1)} %copy.9.rows, s32[8]{0:T(128)S(1)} %bitcast.12, bf16[24,128,128]{2,1,0:T(8,128)(2,1)S(1)} %bitcast.10, bf16[27,128,128]{2,1,0:T(8,128)(2,1)S(1)} %bitcast.8, bf16[27,128,128]{2,1,0:T(8,128)(2,1)S(1)} %bitcast.9, ...), custom_call_target="tpu_custom_call" | custom-call | tf_op jit(solution)/shard_map/pallas_call | solution.py:204
  45.1 0.9 %copy.11 = bf16[1,24,128,128]{3,2,1,0:T(8,128)(2,1)} copy(bf16[1,24,128,128]{3,2,1,0:T(8,128)(2,1)S(1)} %bitcast.7) | data formatting | bytes 1572864
Async XLA Ops:
  0.0 0.8 %copy-start.5 = (s32[1,27,24]{1,2,0:T(8,128)S(1)}, s32[1,27,24]{1,2,0:T(8,128)}, u32[]{:S(2)}) copy-start(s32[1,27,24]{1,2,0:T(8,128)} %param.13) | copy-start | bytes 7780
  0.9 0.7 %copy-start.4 = (s32[1,8]{1,0:T(1,128)S(1)}, s32[1,8]{1,0:T(1,128)}, u32[]{:S(2)}) copy-start(s32[1,8]{1,0:T(1,128)} %param.12) | copy-start | bytes 100
  1.5 1.2 %copy-start = (bf16[1,27,128,128]{3,2,1,0:T(8,128)(2,1)S(1)}, bf16[1,27,128,128]{3,2,1,0:T(8,128)(2,1)}, u32[]{:S(2)}) copy-start(bf16[1,27,128,128]{3,2,1,0:T(8,128)(2,1)} %param.8) | copy-start | bytes 2654212
  2.7 1.2 %copy-start.1 = (bf16[1,27,128,128]{3,2,1,0:T(8,128)(2,1)S(1)}, bf16[1,27,128,128]{3,2,1,0:T(8,128)(2,1)}, u32[]{:S(2)}) copy-start(bf16[1,27,128,128]{3,2,1,0:T(8,128)(2,1)} %param.9) | copy-start | bytes 2654212
  3.9 1.2 %copy-start.2 = (bf16[27,128,128]{2,1,0:T(8,128)(2,1)S(1)}, bf16[27,128,128]{2,1,0:T(8,128)(2,1)}, u32[]{:S(2)}) copy-start(bf16[27,128,128]{2,1,0:T(8,128)(2,1)} %w3_hbm.1) | copy-start | bytes 2654212
  5.0 1.1 %copy-start.3 = (bf16[1,24,128,128]{3,2,1,0:T(8,128)(2,1)S(1)}, bf16[1,24,128,128]{3,2,1,0:T(8,128)(2,1)}, u32[]{:S(2)}) copy-start(bf16[1,24,128,128]{3,2,1,0:T(8,128)(2,1)} %param.7) | copy-start | bytes 2359300

commit v3 on v2

--- a/solution.py
+++ b/solution.py
@@ -11,23 +11,26 @@
 step_cols = (-1, 0, 1, -1, 1, -1, 0, 1)
 
 
-def conv_tiles(ids, pairs, emit, tiles, koff):
+def conv_pair(ids, w, table, first, second):
+    koff = w.shape[0]
+    acc = None
+    for i in range(0, koff, 2):
+        lhs, rhs = [], []
+        for k in range(i, min(i + 2, koff)):
+            lhs.append(w[k])
+            rhs.append(jnp.concatenate([table[ids[k, first]], table[ids[k, second]]], axis=1))
+        part = jnp.dot(
+            jnp.concatenate(lhs, axis=1),
+            jnp.concatenate(rhs, axis=0),
+            preferred_element_type=jnp.float32,
+        )
+        acc = part if acc is None else acc + part
+    return acc
+
+
+def conv_tiles(ids, w, table, emit, tiles):
     def body(step, _):
-        t = step * 2
-        terms = [(w, table, k) for k in range(koff) for w, table in pairs]
-        acc = None
-        for i in range(0, len(terms), 2):
-            lhs, rhs = [], []
-            for w, table, k in terms[i : i + 2]:
-                lhs.append(w[k])
-                rhs.append(jnp.concatenate([table[ids[k, t]], table[ids[k, t + 1]]], axis=1))
-            part = jnp.dot(
-                jnp.concatenate(lhs, axis=1),
-                jnp.concatenate(rhs, axis=0),
-                preferred_element_type=jnp.float32,
-            )
-            acc = part if acc is None else acc + part
-        emit(t, acc)
+        emit(step * 2, conv_pair(ids, w, table, step * 2, step * 2 + 1))
         return 0
 
     lax.fori_loop(0, tiles // 2, body, 0)
@@ -44,7 +47,6 @@
 ):
     tiles, _, vox = feats.shape
     dirs, cap = rows.shape
-    koff = w1.shape[0]
     section = lax.axis_index("section")
     me = lax.axis_index("space")
     grid_a = lax.axis_size("space") // GRID_B
@@ -151,8 +153,31 @@
         def _():
             skip_copy(t).start()
 
-    conv_tiles(ids, [(w1, table1)], emit_first, tiles, koff)
-    halo_send(table2, *halo2)
+    def send_first(d, _):
+        step = d + jnp.where(d >= dirs // 2, 1, 0).astype(jnp.int32)
+        da, db = step // 3 - 1, step % 3 - 1
+        r, c = row + da, col + db
+
+        @pl.when((r >= 0) & (r < grid_a) & (c >= 0) & (c < GRID_B))
+        def _():
+            part = conv_pair(ids, w1, table1, rows[d, 0], rows[d, 1])
+            part = jnp.maximum(part, 0.0).astype(outbox2.dtype)
+            for j in range(cap):
+                tile = part[:, j * vox : (j + 1) * vox]
+                outbox2[d, j] = jnp.where(j < counts[d], tile, jnp.zeros_like(tile))
+            pltpu.make_async_remote_copy(
+                src_ref=outbox2.at[d],
+                dst_ref=inbox2.at[d],
+                send_sem=send2.at[d],
+                recv_sem=recv2.at[d],
+                device_id={"section": section, "space": me + da * GRID_B + db},
+                device_id_type=MESH,
+            ).start()
+
+        return 0
+
+    lax.fori_loop(0, dirs, send_first, 0)
+    conv_tiles(ids, w1, table1, emit_first, tiles)
 
     @pl.when(section == 1)
     def _():
@@ -169,7 +194,7 @@
         out[t] = part[:, :vox]
         out[t + 1] = part[:, vox:]
 
-    conv_tiles(ids, [(w2, table2)], emit_out, tiles, koff)
+    conv_tiles(ids, w2, table2, emit_out, tiles)
 
     @pl.when(section == 0)
     def _():
@@ -184,7 +209,7 @@
             out[t] = part[:, :vox]
             out[t + 1] = part[:, vox:]
 
-        conv_tiles(ids, [(w3, table3)], emit_sum, tiles, koff)
+        conv_tiles(ids, w3, table3, emit_sum, tiles)
         halo_sent(*halo3)
 
     halo_sent(*halo1)

time: 46.3 us -> 43.8 us (0.946)
  the two profiles are of different devices: /device:TPU:31 before, /device:TPU:5 now
where the time goes in v3:
time: 43.8 us; the launch traced here: 43.5 us
  Pallas kernels  36.5 us (83%)
  local copies, waits for them, and re-layouts  7.03 us (16%)
    pallas_call x1, Pallas kernels, local(): pl.pallas_call(network, out_shape=jax.ShapeDtypeStruct((tiles, channels,...  36.5 us
    unnamed x14, local copies, waits for them, and re-layouts  6.26 us

profile of v3, /device:TPU:5, one launch (start us, length us, event | category | flops | bytes accessed | tf_op | source)
XLA Modules:
  0.0 43.5 jit_solution(11647814918175129590)
XLA Ops:
  0.0 0.0 copy-start.5
  0.0 0.8 %copy.9.rows = s32[8,2]{1,0:T(8,128)S(1)} copy(s32[8,2]{0,1:T(2,128)} %bitcast.13) | data formatting | bytes 128 | tf_op jit(solution)/shard_map/squeeze | solution.py:220
  0.8 0.0 copy-done.5
  0.8 0.1 copy.8
  0.9 0.0 copy-start.4
  0.9 0.7 %copy-done.4 = s32[1,8]{1,0:T(1,128)S(1)} copy-done((s32[1,8]{1,0:T(1,128)S(1)}, s32[1,8]{1,0:T(1,128)}, u32[]{:S(2)}) %copy-start.4) | copy-done | bytes 56
  1.5 0.0 copy-start
  1.5 1.2 %copy-done = bf16[1,27,128,128]{3,2,1,0:T(8,128)(2,1)S(1)} copy-done((bf16[1,27,128,128]{3,2,1,0:T(8,128)(2,1)S(1)}, bf16[1,27,128,128]{3,2,1,0:T(8,128)(2,1)}, u32[]{:S(2)}) %copy-start) | copy-done | bytes 884760
  2.7 0.0 copy-start.1
  2.7 1.2 %copy-done.1 = bf16[1,27,128,128]{3,2,1,0:T(8,128)(2,1)S(1)} copy-done((bf16[1,27,128,128]{3,2,1,0:T(8,128)(2,1)S(1)}, bf16[1,27,128,128]{3,2,1,0:T(8,128)(2,1)}, u32[]{:S(2)}) %copy-start.1) | copy-done | bytes 884760
  3.9 0.0 copy-start.2
  3.9 1.2 %copy-done.2 = bf16[27,128,128]{2,1,0:T(8,128)(2,1)S(1)} copy-done((bf16[27,128,128]{2,1,0:T(8,128)(2,1)S(1)}, bf16[27,128,128]{2,1,0:T(8,128)(2,1)}, u32[]{:S(2)}) %copy-start.2) | copy-done | bytes 884760
  5.0 0.0 copy-start.3
  5.0 1.1 %copy-done.3 = bf16[1,24,128,128]{3,2,1,0:T(8,128)(2,1)S(1)} copy-done((bf16[1,24,128,128]{3,2,1,0:T(8,128)(2,1)S(1)}, bf16[1,24,128,128]{3,2,1,0:T(8,128)(2,1)}, u32[]{:S(2)}) %copy-start.3) | copy-done | bytes 786456
  6.2 36.5 %shard_map.73 = bf16[24,128,128]{2,1,0:T(8,128)(2,1)S(1)} custom-call(s32[27,24]{1,0:T(8,128)S(1)} %bitcast.11, s32[8,2]{1,0:T(8,128)S(1)} %copy.9.rows, s32[8]{0:T(128)S(1)} %bitcast.12, bf16[24,128,128]{2,1,0:T(8,128)(2,1)S(1)} %bitcast.10, bf16[27,128,128]{2,1,0:T(8,128)(2,1)S(1)} %bitcast.8, bf16[27,128,128]{2,1,0:T(8,128)(2,1)S(1)} %bitcast.9, ...), custom_call_target="tpu_custom_call" | custom-call | tf_op jit(solution)/shard_map/pallas_call | solution.py:229
  42.6 0.9 %copy.11 = bf16[1,24,128,128]{3,2,1,0:T(8,128)(2,1)} copy(bf16[1,24,128,128]{3,2,1,0:T(8,128)(2,1)S(1)} %bitcast.7) | data formatting | bytes 1572864
Async XLA Ops:
  0.0 0.8 %copy-start.5 = (s32[1,27,24]{1,2,0:T(8,128)S(1)}, s32[1,27,24]{1,2,0:T(8,128)}, u32[]{:S(2)}) copy-start(s32[1,27,24]{1,2,0:T(8,128)} %param.13) | copy-start | bytes 7780
  0.9 0.7 %copy-start.4 = (s32[1,8]{1,0:T(1,128)S(1)}, s32[1,8]{1,0:T(1,128)}, u32[]{:S(2)}) copy-start(s32[1,8]{1,0:T(1,128)} %param.12) | copy-start | bytes 100
  1.5 1.2 %copy-start = (bf16[1,27,128,128]{3,2,1,0:T(8,128)(2,1)S(1)}, bf16[1,27,128,128]{3,2,1,0:T(8,128)(2,1)}, u32[]{:S(2)}) copy-start(bf16[1,27,128,128]{3,2,1,0:T(8,128)(2,1)} %param.8) | copy-start | bytes 2654212
  2.7 1.2 %copy-start.1 = (bf16[1,27,128,128]{3,2,1,0:T(8,128)(2,1)S(1)}, bf16[1,27,128,128]{3,2,1,0:T(8,128)(2,1)}, u32[]{:S(2)}) copy-start(bf16[1,27,128,128]{3,2,1,0:T(8,128)(2,1)} %param.9) | copy-start | bytes 2654212
  3.9 1.2 %copy-start.2 = (bf16[27,128,128]{2,1,0:T(8,128)(2,1)S(1)}, bf16[27,128,128]{2,1,0:T(8,128)(2,1)}, u32[]{:S(2)}) copy-start(bf16[27,128,128]{2,1,0:T(8,128)(2,1)} %w3_hbm.1) | copy-start | bytes 2654212
  5.0 1.1 %copy-start.3 = (bf16[1,24,128,128]{3,2,1,0:T(8,128)(2,1)S(1)}, bf16[1,24,128,128]{3,2,1,0:T(8,128)(2,1)}, u32[]{:S(2)}) copy-start(bf16[1,24,128,128]{3,2,1,0:T(8,128)(2,1)} %param.7) | copy-start | bytes 2359300

commit v4 on v3

--- a/solution.py
+++ b/solution.py
@@ -18,7 +18,7 @@
         lhs, rhs = [], []
         for k in range(i, min(i + 2, koff)):
             lhs.append(w[k])
-            rhs.append(jnp.concatenate([table[ids[k, first]], table[ids[k, second]]], axis=1))
+            rhs.append(jnp.concatenate([table[ids[first, k]], table[ids[second, k]]], axis=1))
         part = jnp.dot(
             jnp.concatenate(lhs, axis=1),
             jnp.concatenate(rhs, axis=0),
@@ -46,7 +46,7 @@
     local_sems, send1, recv1, send2, recv2, send3, recv3, send_skip, recv_skip,
 ):
     tiles, _, vox = feats.shape
-    dirs, cap = rows.shape
+    cap, dirs = rows.shape
     section = lax.axis_index("section")
     me = lax.axis_index("space")
     grid_a = lax.axis_size("space") // GRID_B
@@ -96,7 +96,7 @@
     def halo_send(table, outbox, inbox, send, recv):
         for d in range(dirs):
             for j in range(cap):
-                tile = table[rows[d, j]]
+                tile = table[rows[j, d]]
                 outbox[d, j] = jnp.where(j < counts[d], tile, jnp.zeros_like(tile))
 
             @pl.when(inside(d, 1))
@@ -160,7 +160,7 @@
 
         @pl.when((r >= 0) & (r < grid_a) & (c >= 0) & (c < GRID_B))
         def _():
-            part = conv_pair(ids, w1, table1, rows[d, 0], rows[d, 1])
+            part = conv_pair(ids, w1, table1, rows[0, d], rows[1, d])
             part = jnp.maximum(part, 0.0).astype(outbox2.dtype)
             for j in range(cap):
                 tile = part[:, j * vox : (j + 1) * vox]
@@ -225,7 +225,7 @@
     weights = pltpu.VMEM(w_skip.shape, w_skip.dtype)
     box = pltpu.VMEM((dirs, cap, channels, vox), own.dtype)
     smem = pl.BlockSpec(memory_space=pltpu.SMEM)
-    anywhere = pl.BlockSpec(memory_space=pl.ANY)
+    anywhere = pl.BlockSpec(memory_space=pltpu.HBM)
     second = pl.pallas_call(
         network,
         out_shape=jax.ShapeDtypeStruct((tiles, channels, vox), own.dtype),
@@ -239,9 +239,9 @@
         + [pltpu.SemaphoreType.DMA((dirs,))] * 6
         + [pltpu.SemaphoreType.DMA((tiles // 2,))] * 2,
         compiler_params=pltpu.CompilerParams(
-            collective_id=0, has_side_effects=True, vmem_limit_bytes=40 * 2**20
+            collective_id=0, has_side_effects=True, vmem_limit_bytes=56 * 2**20
         ),
-    )(ids, send_rows, counts, own, w_first[0], w_second[0], w_skip)
+    )(ids.T, send_rows.T, counts, own, w_first[0], w_second[0], w_skip)
     return second[None]
 
 

time: 43.8 us -> 38.9 us (0.89)
  local copies, waits for them, and re-layouts: 7.03 us -> 2.09 us
    unnamed x14 -> x1, local copies, waits for them, and re-layouts: 6.26 us -> 2.09 us
    squeeze x1 -> x0, local copies, waits for them, and re-layouts: 0.77 us -> none  [local(): ids, send_rows, counts = (neighbours[0], send_tiles[0], send_counts[0])]
where the time goes in v4:
time: 38.9 us; the launch traced here: 38.6 us
  Pallas kernels  36.5 us (94%)
  local copies, waits for them, and re-layouts  2.09 us (5%)
    pallas_call x1, Pallas kernels, local(): pl.pallas_call(network, out_shape=jax.ShapeDtypeStruct((tiles, channels,...  36.5 us
    unnamed x1, local copies, waits for them, and re-layouts  2.09 us

profile of v4, /device:TPU:5, one launch (start us, length us, event | category | flops | bytes accessed | tf_op | source)
XLA Modules:
  0.0 38.6 jit_solution(5650181043632231394)
XLA Ops:
  0.0 36.5 %shard_map.73 = bf16[24,128,128]{2,1,0:T(8,128)(2,1)} custom-call(s32[24,27]{1,0:T(8,128)} %bitcast.15, s32[2,8]{1,0:T(2,128)} %bitcast.16, s32[8]{0:T(128)} %bitcast.17, bf16[24,128,128]{2,1,0:T(8,128)(2,1)} %bitcast.14, bf16[27,128,128]{2,1,0:T(8,128)(2,1)} %bitcast.12, bf16[27,128,128]{2,1,0:T(8,128)(2,1)} %bitcast.13, bf16[27,128,128]{2,1,0:T(8,128)(2,1)} %w3_hbm.1), custom_call_target="tpu_custom_call" | custom-call | tf_op jit(solution)/shard_map/pallas_call | solution.py:229
  36.6 2.1 %copy.9 = bf16[1,24,128,128]{3,2,1,0:T(8,128)(2,1)} copy(bf16[1,24,128,128]{3,2,1,0:T(8,128)(2,1)} %bitcast.11) | data formatting | bytes 1572864

commit v5 on v4

--- a/solution.py
+++ b/solution.py
@@ -29,11 +29,16 @@
 
 
 def conv_tiles(ids, w, table, emit, tiles):
+    width = 4 if tiles % 4 == 0 else 2
+
     def body(step, _):
-        emit(step * 2, conv_pair(ids, w, table, step * 2, step * 2 + 1))
+        firsts = [step * width + i for i in range(0, width, 2)]
+        parts = [conv_pair(ids, w, table, t, t + 1) for t in firsts]
+        for t, part in zip(firsts, parts):
+            emit(t, part)
         return 0
 
-    lax.fori_loop(0, tiles // 2, body, 0)
+    lax.fori_loop(0, tiles // width, body, 0)
 
 
 MESH = pl.DeviceIdType.MESH
@@ -94,7 +99,7 @@
         )
 
     def halo_send(table, outbox, inbox, send, recv):
-        for d in range(dirs):
+        for d in sorted(range(dirs), key=lambda d: step_rows[d] == 0):
             for j in range(cap):
                 tile = table[rows[j, d]]
                 outbox[d, j] = jnp.where(j < counts[d], tile, jnp.zeros_like(tile))

time: 38.9 us -> 36.2 us (0.931)
  Pallas kernels: 36.5 us -> 33.5 us
    pallas_call x1, Pallas kernels: 36.5 us -> 33.5 us  [local(): pl.pallas_call(network, out_shape=jax.ShapeDtypeStruct((tiles, channels,...]
where the time goes in v5:
time: 36.2 us; the launch traced here: 35.6 us
  Pallas kernels  33.5 us (93%)
  local copies, waits for them, and re-layouts  2.09 us (6%)
    pallas_call x1, Pallas kernels, local(): pl.pallas_call(network, out_shape=jax.ShapeDtypeStruct((tiles, channels,...  33.5 us
    unnamed x1, local copies, waits for them, and re-layouts  2.09 us

profile of v5, /device:TPU:5, one launch (start us, length us, event | category | flops | bytes accessed | tf_op | source)
XLA Modules:
  0.0 35.6 jit_solution(9651052496616065528)
XLA Ops:
  0.0 33.5 %shard_map.73 = bf16[24,128,128]{2,1,0:T(8,128)(2,1)} custom-call(s32[24,27]{1,0:T(8,128)} %bitcast.15, s32[2,8]{1,0:T(2,128)} %bitcast.16, s32[8]{0:T(128)} %bitcast.17, bf16[24,128,128]{2,1,0:T(8,128)(2,1)} %bitcast.14, bf16[27,128,128]{2,1,0:T(8,128)(2,1)} %bitcast.12, bf16[27,128,128]{2,1,0:T(8,128)(2,1)} %bitcast.13, bf16[27,128,128]{2,1,0:T(8,128)(2,1)} %w3_hbm.1), custom_call_target="tpu_custom_call" | custom-call | tf_op jit(solution)/shard_map/pallas_call | solution.py:234
  33.5 2.1 %copy.9 = bf16[1,24,128,128]{3,2,1,0:T(8,128)(2,1)} copy(bf16[1,24,128,128]{3,2,1,0:T(8,128)(2,1)} %bitcast.11) | data formatting | bytes 1572864

commit v6 on v5

--- a/solution.py
+++ b/solution.py
@@ -181,8 +181,15 @@
 
         return 0
 
-    lax.fori_loop(0, dirs, send_first, 0)
+    @pl.when(section == 1)
+    def _():
+        lax.fori_loop(0, dirs, send_first, 0)
+
     conv_tiles(ids, w1, table1, emit_first, tiles)
+
+    @pl.when(section == 0)
+    def _():
+        lax.fori_loop(0, dirs, send_first, 0)
 
     @pl.when(section == 1)
     def _():

time: 36.2 us -> 37.4 us (1.033)
  the two profiles are of different devices: /device:TPU:5 before, /device:TPU:7 now
where the time goes in v6:
time: 37.4 us; the launch traced here: 37.2 us
  Pallas kernels  35.1 us (94%)
  local copies, waits for them, and re-layouts  2.09 us (6%)
    pallas_call x1, Pallas kernels, local(): pl.pallas_call(network, out_shape=jax.ShapeDtypeStruct((tiles, channels,...  35.1 us
    unnamed x1, local copies, waits for them, and re-layouts  2.09 us

profile of v6, /device:TPU:7, one launch (start us, length us, event | category | flops | bytes accessed | tf_op | source)
XLA Modules:
  0.0 37.2 jit_solution(2788037567724394950)
XLA Ops:
  0.0 35.1 %shard_map.73 = bf16[24,128,128]{2,1,0:T(8,128)(2,1)} custom-call(s32[24,27]{1,0:T(8,128)} %bitcast.15, s32[2,8]{1,0:T(2,128)} %bitcast.16, s32[8]{0:T(128)} %bitcast.17, bf16[24,128,128]{2,1,0:T(8,128)(2,1)} %bitcast.14, bf16[27,128,128]{2,1,0:T(8,128)(2,1)} %bitcast.12, bf16[27,128,128]{2,1,0:T(8,128)(2,1)} %bitcast.13, bf16[27,128,128]{2,1,0:T(8,128)(2,1)} %w3_hbm.1), custom_call_target="tpu_custom_call" | custom-call | tf_op jit(solution)/shard_map/pallas_call | solution.py:241
  35.1 2.1 %copy.9 = bf16[1,24,128,128]{3,2,1,0:T(8,128)(2,1)} copy(bf16[1,24,128,128]{3,2,1,0:T(8,128)(2,1)} %bitcast.11) | data formatting | bytes 1572864

commit v7 on v5

--- a/solution.py
+++ b/solution.py
@@ -29,7 +29,7 @@
 
 
 def conv_tiles(ids, w, table, emit, tiles):
-    width = 4 if tiles % 4 == 0 else 2
+    width = 8 if tiles % 8 == 0 else 2
 
     def body(step, _):
         firsts = [step * width + i for i in range(0, width, 2)]

time: 36.2 us -> 36 us (level)
  the two profiles are of different devices: /device:TPU:5 before, /device:TPU:9 now
where the time goes in v7:
time: 36 us; the launch traced here: 35.8 us
  Pallas kernels  33.7 us (94%)
  local copies, waits for them, and re-layouts  2.09 us (6%)
    pallas_call x1, Pallas kernels, local(): pl.pallas_call(network, out_shape=jax.ShapeDtypeStruct((tiles, channels,...  33.7 us
    unnamed x1, local copies, waits for them, and re-layouts  2.09 us

profile of v7, /device:TPU:9, one launch (start us, length us, event | category | flops | bytes accessed | tf_op | source)
XLA Modules:
  0.0 35.8 jit_solution(16545631874387150910)
XLA Ops:
  0.0 33.7 %shard_map.73 = bf16[24,128,128]{2,1,0:T(8,128)(2,1)} custom-call(s32[24,27]{1,0:T(8,128)} %bitcast.15, s32[2,8]{1,0:T(2,128)} %bitcast.16, s32[8]{0:T(128)} %bitcast.17, bf16[24,128,128]{2,1,0:T(8,128)(2,1)} %bitcast.14, bf16[27,128,128]{2,1,0:T(8,128)(2,1)} %bitcast.12, bf16[27,128,128]{2,1,0:T(8,128)(2,1)} %bitcast.13, bf16[27,128,128]{2,1,0:T(8,128)(2,1)} %w3_hbm.1), custom_call_target="tpu_custom_call" | custom-call | tf_op jit(solution)/shard_map/pallas_call | solution.py:234
  33.7 2.1 %copy.9 = bf16[1,24,128,128]{3,2,1,0:T(8,128)(2,1)} copy(bf16[1,24,128,128]{3,2,1,0:T(8,128)(2,1)} %bitcast.11) | data formatting | bytes 1572864

commit v8 on v7

--- a/solution.py
+++ b/solution.py
@@ -158,7 +158,8 @@
         def _():
             skip_copy(t).start()
 
-    def send_first(d, _):
+    def send_first(i, _):
+        d = jnp.where(i < 3, i, jnp.where(i < 6, i + 2, i - 3)).astype(jnp.int32)
         step = d + jnp.where(d >= dirs // 2, 1, 0).astype(jnp.int32)
         da, db = step // 3 - 1, step % 3 - 1
         r, c = row + da, col + db

time: 36 us -> 37.4 us (1.039)
  the two profiles are of different devices: /device:TPU:9 before, /device:TPU:15 now
where the time goes in v8:
time: 37.4 us; the launch traced here: 37.2 us
  Pallas kernels  35.1 us (94%)
  local copies, waits for them, and re-layouts  2.09 us (6%)
    pallas_call x1, Pallas kernels, local(): pl.pallas_call(network, out_shape=jax.ShapeDtypeStruct((tiles, channels,...  35.1 us
    unnamed x1, local copies, waits for them, and re-layouts  2.09 us

profile of v8, /device:TPU:15, one launch (start us, length us, event | category | flops | bytes accessed | tf_op | source)
XLA Modules:
  0.0 37.2 jit_solution(5406569812312950855)
XLA Ops:
  0.0 35.1 %shard_map.73 = bf16[24,128,128]{2,1,0:T(8,128)(2,1)} custom-call(s32[24,27]{1,0:T(8,128)} %bitcast.15, s32[2,8]{1,0:T(2,128)} %bitcast.16, s32[8]{0:T(128)} %bitcast.17, bf16[24,128,128]{2,1,0:T(8,128)(2,1)} %bitcast.14, bf16[27,128,128]{2,1,0:T(8,128)(2,1)} %bitcast.12, bf16[27,128,128]{2,1,0:T(8,128)(2,1)} %bitcast.13, bf16[27,128,128]{2,1,0:T(8,128)(2,1)} %w3_hbm.1), custom_call_target="tpu_custom_call" | custom-call | tf_op jit(solution)/shard_map/pallas_call | solution.py:235
  35.1 2.1 %copy.9 = bf16[1,24,128,128]{3,2,1,0:T(8,128)(2,1)} copy(bf16[1,24,128,128]{3,2,1,0:T(8,128)(2,1)} %bitcast.11) | data formatting | bytes 1572864
